TPU v7x, 256 devices: a whole 4x4x8 slice. The times are simulated.
256 devices in a mesh: patch: 32 (over y, z), req: 4 (over x), owner: 2 (over core).
Axes of the slice: x: 4, y: 4, z: 8, core: 2. Of those that a mesh axis runs over, the one named last changes fastest.
Arguments:
- latents: bfloat16 [8, 256, 256, 320], P('req', 'patch', 'owner'), may hold values from -24 to 24
- timestep_embedding: bfloat16 [8, 1280], P('req'), may hold values from -6 to 6
- embedding_weight: bfloat16 [1280, 320], replicated, may hold values from -0.15625 to 0.15625
- group_norm_gain: float32 [2, 320], replicated, may hold values from 0.25 to 1.75
- group_norm_shift: float32 [2, 320], replicated, may hold values from -3 to 3
- kernel_weight: bfloat16 [2, 9, 320, 320], replicated, may hold values from -0.109375 to 0.109375
- plugin_reduce_library: bfloat16 [8, 2, 184320], P(('req', 'owner'), None, 'patch'), may hold values from -0.109375 to 0.109375
- plugin_expand_library: bfloat16 [8, 2, 20480], P(('req', 'owner'), None, 'patch'), may hold values from -0.75 to 0.75
- image_adapter: int32 [8, 1], P('req'), may hold values from 0 to 7
- adapter_bank_row: int32 [8], replicated, may hold values from 0 to 7, each once
Outputs:
- result: bfloat16 [8, 256, 256, 320], P('req', 'patch', 'owner')
Inputs may be any that keep to these rules, and one draw needn't show every extreme that they name: `image_adapter`: each image names one adapter; every adapter is named by some image. A permutation: adapter a is stored in bank row adapter_bank_row[a].
All inputs are finite; a program needn't handle non-finite values.
Results may differ from a plain program's by a relative error of at most 0.0055.
Values may be sent and summed in bfloat16 or wider, within the bound.
A program may use at most 128 MiB of HBM per device.

v0:
```python
import jax
import jax.numpy as jnp
from jax import lax
from jax.sharding import PartitionSpec as P

GROUPS = 32


def padded_2(block, sides, width):
    for axis, dim in sides:
        count = lax.axis_size(axis)
        forward = [(i, i + 1) for i in range(count - 1)]
        backward = [(target, source) for source, target in forward]
        low = lax.ppermute(
            lax.slice_in_dim(block, block.shape[dim] - width, None, axis=dim), axis, forward
        )
        high = lax.ppermute(lax.slice_in_dim(block, 0, width, axis=dim), axis, backward)
        block = jnp.concatenate([low, block, high], axis=dim)
    return block


def group_act(values, gain, shift):
    images, rows, columns, chans = values.shape
    grouped = values.reshape(images, rows, columns, GROUPS, chans // GROUPS)
    count = rows * columns * (chans // GROUPS) * lax.axis_size("patch") * lax.axis_size("owner")
    total = lax.psum(jnp.sum(grouped, axis=(1, 2, 4)), ("patch", "owner"))
    mean = total / count
    centered = grouped - mean[:, None, None, :, None]
    spread = lax.psum(jnp.sum(centered * centered, axis=(1, 2, 4)), ("patch", "owner"))
    var = spread / count
    normed = (centered / jnp.sqrt(var + 1e-05)[:, None, None, :, None]).reshape(values.shape)
    return jax.nn.silu(normed * gain + shift).astype(jnp.bfloat16)


def block_conv(act, kernel, reducing_filter, expanding_linear_map):
    images, rows, columns, chans = act.shape
    outward = kernel.shape[2]
    padded = padded_2(act, (("patch", 1), ("owner", 2)), 1)
    joined = jnp.concatenate(
        [jnp.broadcast_to(kernel[None], (images,) + kernel.shape), reducing_filter], axis=3
    )
    accum = jnp.zeros((images, rows, columns, joined.shape[3]), jnp.float32)
    for tap in range(9):
        row_off, col_off = divmod(tap, 3)
        window = padded[:, row_off : row_off + rows, col_off : col_off + columns, :]
        accum = accum + jnp.einsum(
            "bhwc,bcd->bhwd", window, joined[:, tap], preferred_element_type=jnp.float32
        )
    lowpart = accum[..., outward:].astype(jnp.bfloat16)
    return accum[..., :outward] + jnp.einsum(
        "bhwr,brd->bhwd", lowpart, expanding_linear_map, preferred_element_type=jnp.float32
    )


def local(
    latents,
    timestep_embedding,
    embedding_weight,
    group_norm_gain,
    group_norm_shift,
    kernel_weight,
    plugin_reduce_library,
    plugin_expand_library,
    image_adapter,
    adapter_bank_row,
):
    images, rows, columns, chans = latents.shape
    wanted = image_adapter[:, 0]
    table = jnp.arange(adapter_bank_row.shape[0], dtype=jnp.int32)
    slots = jnp.sum(
        jnp.where(wanted[:, None] == table[None, :], adapter_bank_row[None, :], 0), axis=1
    )
    full_down, full_up = (
        lax.all_gather(plugin_reduce_library, "patch", axis=2, tiled=True),
        lax.all_gather(plugin_expand_library, "patch", axis=2, tiled=True),
    )
    pieces = (
        lax.all_gather(full_down, ("req", "owner"), axis=0, tiled=True),
        lax.all_gather(full_up, ("req", "owner"), axis=0, tiled=True),
    )
    count = pieces[0].shape[0]
    match = (slots[:, None] == jnp.arange(count, dtype=jnp.int32)[None, :]).astype(jnp.bfloat16)
    first = jnp.einsum("ik,kjs->ijs", match, pieces[0], preferred_element_type=jnp.float32)
    second = jnp.einsum("ik,kjs->ijs", match, pieces[1], preferred_element_type=jnp.float32)
    down_sel = first.astype(jnp.bfloat16)
    up_sel = second.astype(jnp.bfloat16)
    rank = up_sel.shape[2] // chans
    down_all = down_sel.reshape(images, 2, 9, chans, rank)
    up_all = up_sel.reshape(images, 2, rank, chans)
    temb = jax.nn.silu(timestep_embedding.astype(jnp.float32)).astype(jnp.bfloat16)
    proj = jnp.dot(temb, embedding_weight, preferred_element_type=jnp.float32)
    source = latents.astype(jnp.float32)
    act1 = group_act(source, group_norm_gain[0], group_norm_shift[0])
    hidden1 = (
        block_conv(act1, kernel_weight[0], down_all[:, 0], up_all[:, 0]) + proj[:, None, None, :]
    ).astype(jnp.bfloat16)
    act2 = group_act(hidden1.astype(jnp.float32), group_norm_gain[1], group_norm_shift[1])
    result = source + block_conv(act2, kernel_weight[1], down_all[:, 1], up_all[:, 1])
    return result.astype(jnp.bfloat16)


def solution(mesh):
    in_specs = (
        P("req", "patch", "owner", None),
        P("req", None),
        P(),
        P(),
        P(),
        P(),
        P(("req", "owner"), None, "patch"),
        P(("req", "owner"), None, "patch"),
        P("req", None),
        P(),
    )
    out_specs = P("req", "patch", "owner", None)
    return jax.shard_map(local, mesh=mesh, in_specs=in_specs, out_specs=out_specs, check_vma=False)
```

profile of v0, /device:TPU:1, one launch (start us, length us, event | category | flops | bytes accessed | tf_op | source)
XLA Modules:
  0.0 778.4 jit_solution(10491722644223189108)
XLA Ops:
  6.6 47.2 %all_gather.12 = bf16[1,2,184320]{2,1,0:T(2,128)(2,1)} all-gather(bf16[1,2,5760]{2,1,0:T(2,128)(2,1)} %param.16), channel_id=1, replica_groups=mesh['patch'=32,'req'=4,'owner'=2] {'patch'}, dimensions={2}, use_global_device_ids=true | all-gather | bytes 760320 | tf_op jit(solution)/shard_map/all_gather | solution.py:74
  55.6 135.6 %psum.28 = f32[2,32]{1,0:T(2,128)S(1)} all-reduce(f32[2,32]{1,0:T(2,128)S(1)} %reduce_sum.59), channel_id=1, replica_groups=mesh['patch'=32,'req'=4,'owner'=2] {'patch','owner'}, use_global_device_ids=true, to_apply=%region_2.3 | all-reduce | flops 64 | bytes 512 | tf_op jit(solution)/shard_map/psum | solution.py:26
  192.2 124.0 %psum.29 = f32[2,32]{1,0:T(2,128)S(1)} all-reduce(f32[2,32]{1,0:T(2,128)S(1)} %reduce_sum.62), channel_id=1, replica_groups=mesh['patch'=32,'req'=4,'owner'=2] {'patch','owner'}, use_global_device_ids=true, to_apply=%region_5.6 | all-reduce | flops 64 | bytes 512 | tf_op jit(solution)/shard_map/psum | solution.py:29
  320.5 32.0 %all_gather.14 = bf16[1,2,20480]{2,1,0:T(2,128)(2,1)S(1)} all-gather(bf16[1,2,640]{2,1,0:T(2,128)(2,1)S(1)} %copy-done.16), channel_id=1, replica_groups=mesh['patch'=32,'req'=4,'owner'=2] {'patch'}, dimensions={2}, use_global_device_ids=true | all-gather | bytes 84480 | tf_op jit(solution)/shard_map/all_gather | solution.py:75
  352.5 24.4 %all_gather.15 = bf16[8,2,20480]{2,1,0:T(2,128)(2,1)S(1)} all-gather(bf16[1,2,20480]{2,1,0:T(2,128)(2,1)S(1)} %all_gather.14), channel_id=1, replica_groups=mesh['patch'=32,'req'=4,'owner'=2] {'req','owner'}, dimensions={0}, use_global_device_ids=true | all-gather | bytes 737280 | tf_op jit(solution)/shard_map/all_gather | solution.py:79
  377.0 4.8 slice_bitcast_fusion
  390.1 3.5 collective-permute-start.3
  398.0 5.7 pad_maximum_fusion
  403.7 10.7 %convolution_convert_fusion = bf16[2,2,184320]{2,0,1:T(2,128)(2,1)} fusion(bf16[8,2,184320]{2,1,0:T(2,128)(2,1)} %all-gather.2.cloned.1.call-done, s32[2]{0:T(128)S(1)} %fusion.123), kind=kOutput, calls=%fused_computation | convolution fusion | flops 12533776 | bytes 7372808 | tf_op jit(solution)/shard_map/ik,kjs->ijs/dot_general | solution.py:83
  414.4 4.7 reshape.54
  419.1 3.3 fusion.145
  428.2 2.9 fusion.54
  431.1 2.9 fusion.50
  439.4 2.7 fusion.14
  444.9 9.6 %add_add_fusion.1 = f32[2,8,128,384]{2,3,1,0:T(8,128)} fusion(f32[2,8,128,384]{2,3,1,0:T(8,128)} %fusion.18, f32[2,8,128,384]{2,3,1,0:T(8,128)} %fusion.48, f32[2,8,128,384]{2,3,1,0:T(8,128)} %fusion.50, f32[2,8,128,384]{2,3,1,0:T(8,128)} %fusion.80, f32[2,8,128,384]{2,3,1,0:T(8,128)S(1)} %copy-done.10, f32[2,8,128,384]{2,3,1,0:T(8,128)} %fusion.54, ...), kind=kOutput, calls=%fused_computation.45 | convolution fusion | flops 510590976 | bytes 35520512 | tf_op jit(solution)/shard_map/bhwc,bcd->bhwd/dot_general | solution.py:46
  457.3 122.8 %psum.30 = f32[2,32]{1,0:T(2,128)S(1)} all-reduce(f32[2,32]{1,0:T(2,128)S(1)} %reduce_sum.82), channel_id=1, replica_groups=mesh['patch'=32,'req'=4,'owner'=2] {'patch','owner'}, use_global_device_ids=true, to_apply=%region_9.10 | all-reduce | flops 64 | bytes 512 | tf_op jit(solution)/shard_map/psum | solution.py:26
  581.0 127.5 %psum.31 = f32[2,32]{1,0:T(2,128)S(1)} all-reduce(f32[2,32]{1,0:T(2,128)S(1)} %reduce_sum.85), channel_id=1, replica_groups=mesh['patch'=32,'req'=4,'owner'=2] {'patch','owner'}, use_global_device_ids=true, to_apply=%region_12.13 | all-reduce | flops 64 | bytes 512 | tf_op jit(solution)/shard_map/psum | solution.py:29
  714.9 3.2 fusion.97
  727.7 3.7 collective-permute-start.7
  731.4 4.1 fusion.22
  741.8 5.0 pad_maximum_fusion.1
  752.2 2.9 fusion.40
  755.1 2.9 fusion.36
  760.7 8.9 %add_add_fusion = f32[2,8,128,384]{2,3,1,0:T(8,128)S(1)} fusion(f32[2,8,128,384]{2,3,1,0:T(8,128)} %fusion.26, f32[2,8,128,384]{2,3,1,0:T(8,128)} %fusion.34, f32[2,8,128,384]{2,3,1,0:T(8,128)} %fusion.36, f32[2,8,128,384]{2,3,1,0:T(8,128)S(1)} %copy-done.9, f32[2,8,128,384]{2,3,1,0:T(8,128)} %fusion.38, f32[2,8,128,384]{2,3,1,0:T(8,128)} %fusion.40, ...), kind=kOutput, calls=%fused_computation.44 | convolution fusion | flops 510590976 | bytes 35520512 | tf_op jit(solution)/shard_map/bhwc,bcd->bhwd/dot_general | solution.py:46
  (124 shorter events, 69.0 us)
Async XLA Ops:
  6.5 375.3 %copy-start = (bf16[1280,320]{0,1:T(8,128)(2,1)S(1)}, bf16[1280,320]{0,1:T(8,128)(2,1)}, u32[]{:S(2)}) copy-start(bf16[1280,320]{0,1:T(8,128)(2,1)} %param.12) | copy-start | bytes 2457604
  6.5 184.9 %copy-start.5 = (bf16[2,8,128,320]{2,3,1,0:T(8,128)(2,1)S(1)}, bf16[2,8,128,320]{2,3,1,0:T(8,128)(2,1)}, u32[]{:S(2)}) copy-start(bf16[2,8,128,320]{2,3,1,0:T(8,128)(2,1)} %param.10) | copy-start | bytes 3932164
  6.5 309.9 %copy-start.15 = (f32[2,320]{1,0:T(2,128)S(1)}, f32[2,320]{1,0:T(2,128)}, u32[]{:S(2)}) copy-start(f32[2,320]{1,0:T(2,128)} %param.13) | copy-start | bytes 7684
  6.5 309.9 %copy-start.14 = (f32[2,320]{1,0:T(2,128)S(1)}, f32[2,320]{1,0:T(2,128)}, u32[]{:S(2)}) copy-start(f32[2,320]{1,0:T(2,128)} %param.14) | copy-start | bytes 7684
  6.5 397.2 %all-gather.2.cloned.1.call-start = ((), (), s32[]{:S(2)}) async-start(), calls=%async_computation | async-start | bytes 6635520 | tf_op jit(solution)/shard_map/all_gather | solution.py:78
  53.8 266.6 %copy-start.16 = (bf16[1,2,640]{2,1,0:T(2,128)(2,1)S(1)}, bf16[1,2,640]{2,1,0:T(2,128)(2,1)}, u32[]{:S(2)}) copy-start(bf16[1,2,640]{2,1,0:T(2,128)(2,1)} %param.17) | copy-start | bytes 7684
  317.9 64.4 %collective-permute-start = (bf16[2,1,128,320]{2,3,1,0:T(8,128)(2,1)S(1)}, bf16[2,1,128,320]{2,3,1,0:T(8,128)(2,1)S(1)}, u32[]{:S(2)}, u32[]{:S(2)}) collective-permute-start(bf16[2,1,128,320]{2,3,1,0:T(8,128)(2,1)S(1)} %get-tuple-element.23), channel_id=1, source_target_pairs={{0,8},{8,16},{16,24},{24,32},{32,40},{40,48},{48,56},{56,64},{64,7... | collective-permute-start | bytes 491528 | tf_op jit(solution)/shard_map/ppermute | solution.py:14
  319.2 63.1 %collective-permute-start.1 = (bf16[2,1,128,320]{2,3,1,0:T(8,128)(2,1)S(1)}, bf16[2,1,128,320]{2,3,1,0:T(8,128)(2,1)S(1)}, u32[]{:S(2)}, u32[]{:S(2)}) collective-permute-start(bf16[2,1,128,320]{2,3,1,0:T(8,128)(2,1)S(1)} %get-tuple-element.24), channel_id=1, source_target_pairs={{8,0},{16,8},{24,16},{32,24},{40,32},{48,40},{56,48},{64,56},{72,6... | collective-permute-start | bytes 491528 | tf_op jit(solution)/shard_map/ppermute | solution.py:17
  377.0 5.1 copy-start.17
  377.0 5.1 copy-start.18
  386.9 7.8 collective-permute-start.2
  390.1 6.3 collective-permute-start.3
  708.7 5.5 copy-start.11
  710.1 9.8 %copy-start.3 = (bf16[2,8,128,320]{2,3,1,0:T(8,128)(2,1)}, bf16[2,8,128,320]{2,3,1,0:T(8,128)(2,1)S(1)}, u32[]{:S(2)}) copy-start(bf16[2,8,128,320]{2,3,1,0:T(8,128)(2,1)S(1)} %multiply_convert_fusion) | copy-start | bytes 3932164
  710.2 7.9 %collective-permute-start.4 = (bf16[2,1,128,320]{2,3,1,0:T(8,128)(2,1)S(1)}, bf16[2,1,128,320]{2,3,1,0:T(8,128)(2,1)S(1)}, u32[]{:S(2)}, u32[]{:S(2)}) collective-permute-start(bf16[2,1,128,320]{2,3,1,0:T(8,128)(2,1)S(1)} %get-tuple-element.21), channel_id=1, source_target_pairs={{0,8},{8,16},{16,24},{24,32},{32,40},{40,48},{48,56},{56,64},{64,7... | collective-permute-start | bytes 491528 | tf_op jit(solution)/shard_map/ppermute | solution.py:14
  712.9 7.0 collective-permute-start.5
  724.4 13.8 %collective-permute-start.6 = (bf16[2,10,1,320]{3,0,2,1:T(2,128)(2,1)S(1)}, bf16[2,10,1,320]{3,0,2,1:T(2,128)(2,1)S(1)}, u32[]{:S(2)}, u32[]{:S(2)}) collective-permute-start(bf16[2,10,1,320]{3,0,2,1:T(2,128)(2,1)S(1)} %copy.104), channel_id=1, source_target_pairs={{0,1},{2,3},{4,5},{6,7},{8,9},{10,11},{12,13},{14,15},{16,17},{18,... | collective-permute-start | bytes 38408 | tf_op jit(solution)/shard_map/ppermute | solution.py:14
  725.7 9.8 %slice-start = ((s8[4423680]{0:T(1024)(128)(4,1)}), s8[229376]{0:T(1024)(128)(4,1)S(1)}, s32[]{:S(2)}) async-start(s8[4423680]{0:T(1024)(128)(4,1)} %bitcast.145), calls=%async_computation.1 | async-start | bytes 458752
  727.7 7.8 %slice-start.1 = ((s8[4423680]{0:T(1024)(128)(4,1)}), s8[4194304]{0:T(1024)(128)(4,1)S(1)}, s32[]{:S(2)}) async-start(s8[4423680]{0:T(1024)(128)(4,1)} %bitcast.145), calls=%async_computation.2 | async-start | bytes 8388608
  727.7 7.8 %copy-start.4 = (bf16[2,8,128,320]{2,3,1,0:T(8,128)(2,1)S(1)}, bf16[2,8,128,320]{2,3,1,0:T(8,128)(2,1)}, u32[]{:S(2)}) copy-start(bf16[2,8,128,320]{2,3,1,0:T(8,128)(2,1)} %copy-done.3) | copy-start | bytes 3932164
  727.7 12.5 %collective-permute-start.7 = (bf16[2,10,1,320]{3,0,2,1:T(2,128)(2,1)S(1)}, bf16[2,10,1,320]{3,0,2,1:T(2,128)(2,1)S(1)}, u32[]{:S(2)}, u32[]{:S(2)}) collective-permute-start(bf16[2,10,1,320]{3,0,2,1:T(2,128)(2,1)S(1)} %copy.109), channel_id=1, source_target_pairs={{1,0},{3,2},{5,4},{7,6},{9,8},{11,10},{13,12},{15,14},{17,16},{19,... | collective-permute-start | bytes 38408 | tf_op jit(solution)/shard_map/ppermute | solution.py:17
  740.1 6.7 slice-start.2
  760.7 8.9 %copy-start.6 = (bf16[2,8,128,320]{2,3,1,0:T(8,128)(2,1)S(1)}, bf16[2,8,128,320]{2,3,1,0:T(8,128)(2,1)}, u32[]{:S(2)}) copy-start(bf16[2,8,128,320]{2,3,1,0:T(8,128)(2,1)} %param.10) | copy-start | bytes 3932164
  760.7 10.6 %copy-start.1 = (bf16[1280,320]{0,1:T(8,128)(2,1)S(1)}, bf16[1280,320]{0,1:T(8,128)(2,1)}, u32[]{:S(2)}) copy-start(bf16[1280,320]{0,1:T(8,128)(2,1)} %param.12) | copy-start | bytes 2457604
  (8 other events, 26.5 us)
Sparse Core Ops, SparseCore 0:
  54.0 51.1 all-gather.1
where the time goes:
time: 784 us; the launch traced here: 778 us
  blocking collectives  614 us (78%)
  matrix products  79 us (10%)
  local copies, waits for them, and re-layouts  37.7 us (5%)
  other arithmetic  17 us (2%)
  starting transfers between devices  15 us (2%)
  between operations  14.1 us (2%)
    psum x2, blocking collectives, group_act(): total = lax.psum(jnp.sum(grouped, axis=(1, 2, 4)), ('patch', 'owner'))  258 us
    psum x2, blocking collectives, group_act(): lax.psum(jnp.sum(centered * centered, axis=(1, 2, 4)), ('patch', 'owner'))  252 us
    dot_general x18, matrix products, block_conv(): jnp.einsum('bhwc,bcd->bhwd', window, joined[:, tap], preferred_element_ty...  62.9 us
    all_gather x1, blocking collectives, local(): lax.all_gather(plugin_reduce_library, 'patch', axis=2, tiled=True)  47.2 us
    all_gather x1, blocking collectives, local(): lax.all_gather(plugin_expand_library, 'patch', axis=2, tiled=True)  32 us
    all_gather x1, blocking collectives, local(): lax.all_gather(full_up, ('req', 'owner'), axis=0, tiled=True)  24.4 us
  transfers between devices with their start and end apart: 9, of which 1 were waited for; matrix products, arithmetic and copies ran while one was open for 5% of the time, Pallas kernels for 0%

commit v1 on v0

v1 whole, which is shorter than its diff:
```python
import functools

import jax
import jax.numpy as jnp
from jax import lax
from jax.experimental import pallas as pl
from jax.experimental.pallas import tpu as pltpu
from jax.sharding import PartitionSpec as P

MESH = pl.DeviceIdType.MESH
F32, BF16 = jnp.float32, jnp.bfloat16
Y, Z = 4, 8
RANK = 64
EDGE = 16
GROUP = 10


def remote(src, dst, send, recv, device):
    return pltpu.make_async_remote_copy(
        src_ref=src, dst_ref=dst, send_sem=send, recv_sem=recv, device_id=device, device_id_type=MESH
    )


def place():
    patch, req, owner = lax.axis_index("patch"), lax.axis_index("req"), lax.axis_index("owner")
    return patch, req, owner, patch // Z, patch % Z


def greet(bank):
    patch, req, owner, y, z = place()
    sem = pltpu.get_barrier_semaphore()
    count = 0

    def signal(device):
        pl.semaphore_signal(sem, inc=1, device_id=device, device_id_type=MESH)

    for k in range(1, 2 * Y):
        g = (y * 2 + owner + k) % (2 * Y)
        signal(((g // 2) * Z + z, req, g % 2))
        count += 1
    for k in range(1, Z):
        signal((y * Z + (z + k) % Z, req, owner))
        count += 1
    for step in (1, Y * Z - 1):
        for other in (owner, 1 - owner):
            signal(((patch + step) % (Y * Z), req, other))
            count += 1
    if bank:
        for k in range(1, 8):
            g = (req * 2 + owner + k) % 8
            signal((patch, g // 2, g % 2))
            count += 1
    pl.semaphore_wait(sem, count)


def start_borders(src, top, bot, col, send, recv):
    patch, req, owner, y, z = place()
    rows = src.shape[1]
    last = Y * Z - 1
    edge = pl.multiple_of((1 - owner) * (src.shape[2] - EDGE), EDGE)
    cols = pl.ds(edge, EDGE)
    down = (patch + 1, req, owner)
    up = (patch - 1, req, owner)
    copies = [
        (patch < last, patch > 0, remote(src.at[:, rows - 1], top, send.at[0], recv.at[0], down)),
        (patch > 0, patch < last, remote(src.at[:, 0], bot, send.at[1], recv.at[1], up)),
        (
            patch < last,
            patch > 0,
            remote(src.at[:, rows - 1, cols], col.at[:, 0], send.at[2], recv.at[2], (patch + 1, req, 1 - owner)),
        ),
        (
            patch > 0,
            patch < last,
            remote(src.at[:, 0, cols], col.at[:, rows + 1], send.at[3], recv.at[3], (patch - 1, req, 1 - owner)),
        ),
        (
            None,
            None,
            remote(src.at[:, :, cols], col.at[:, pl.ds(1, rows)], send.at[4], recv.at[4], (patch, req, 1 - owner)),
        ),
    ]
    for sends, _, copy in copies:
        if sends is None:
            copy.start()
        else:
            pl.when(sends)(copy.start)

    @pl.when(patch == 0)
    def _():
        top[...] = jnp.zeros_like(top)
        col[:, 0] = jnp.zeros_like(col[:, 0])

    @pl.when(patch == last)
    def _():
        bot[...] = jnp.zeros_like(bot)
        col[:, rows + 1] = jnp.zeros_like(col[:, rows + 1])

    return copies


def wait_borders(copies):
    for sends, receives, copy in copies:
        if sends is None:
            copy.wait_send()
            copy.wait_recv()
        else:
            pl.when(sends)(copy.wait_send)
            pl.when(receives)(copy.wait_recv)


def local_stats(rows_of, rows):
    def add(f):
        def step(r, total):
            x = f(rows_of(r).astype(F32))
            return total + jnp.sum(x.reshape(x.shape[0] // 8, 8, x.shape[1]), axis=0)

        return step

    chans = rows_of(0).shape[1]
    count = rows * rows_of(0).shape[0]
    zero = jnp.zeros((8, chans), F32)
    total = lax.fori_loop(0, rows, add(lambda x: x), zero)
    mean = jnp.sum(total, axis=0, keepdims=True) * (1.0 / count)
    spread = lax.fori_loop(0, rows, add(lambda x: (x - mean) * (x - mean)), zero)
    return mean, jnp.sum(spread, axis=0, keepdims=True)


def start_exchange(slots, send, recv, peers):
    copies = [
        remote(slots.at[0], slots.at[k], send.at[k], recv.at[k], peer) for k, peer in enumerate(peers, 1)
    ]
    for copy in copies:
        copy.start()
    return copies


def combine(slots, count):
    values = slots[...]
    total = jnp.sum(values, axis=0)
    mean = total * (1.0 / values.shape[0])
    off = values - mean[None]
    between = jnp.sum(off * off, axis=0)
    return mean[0:2], total[2:4] + count * between[0:2]


def first_peers():
    patch, req, owner, y, z = place()
    peers = []
    for k in range(1, 2 * Y):
        g = (y * 2 + owner + k) % (2 * Y)
        peers.append(((g // 2) * Z + z, req, g % 2))
    return peers


def second_peers():
    patch, req, owner, y, z = place()
    return [(y * Z + (z + k) % Z, req, owner) for k in range(1, Z)]


def group_mean(values, groups):
    high = values.astype(BF16)
    rest = values - high.astype(F32)
    middle = rest.astype(BF16)
    low = (rest - middle.astype(F32)).astype(BF16)
    total = (
        jnp.dot(high, groups, preferred_element_type=F32)
        + jnp.dot(middle, groups, preferred_element_type=F32)
        + jnp.dot(low, groups, preferred_element_type=F32)
    )
    return total * (1.0 / GROUP)


def finish_norm(mean, spread, count, gain, shift):
    chans = mean.shape[1]
    row = lax.broadcasted_iota(jnp.int32, (chans, chans), 0)
    column = lax.broadcasted_iota(jnp.int32, (chans, chans), 1)
    groups = jnp.where((row * 6554) >> 16 == (column * 6554) >> 16, 1.0, 0.0).astype(BF16)
    both = jnp.concatenate([mean, mean, mean, mean], axis=0)
    center = group_mean(both, groups)[0:2]
    off = mean - center
    local = spread * (1.0 / count) + off * off
    var = group_mean(jnp.concatenate([local, local, local, local], axis=0), groups)[0:2]
    scale = gain / jnp.sqrt(var + 1e-05)
    return center, 0.5 * scale, 0.5 * shift


def gather_bank(piece, image_adapter, bank_row, held, lora, send, recv):
    patch, req, owner, y, z = place()
    me = req * 2 + owner
    held[me] = piece[...]
    copies = []
    for k in range(1, 8):
        g = (me + k) % 8
        copy = remote(held.at[me], held.at[me], send.at[k], recv.at[k], (patch, g // 2, g % 2))
        copy.start()
        copies.append(copy)
    for copy in copies:
        copy.wait()
    slot = bank_row[image_adapter[owner, 0]]
    lora[owner, z, y] = held[slot]
    copies = []
    for k in range(1, Y):
        block = lora.at[owner, z, y]
        copy = remote(block, block, send.at[7 + k], recv.at[7 + k], (((y + k) % Y) * Z + z, req, owner))
        copy.start()
        copies.append(copy)
    for copy in copies:
        copy.wait()
    right = (y * Z + (z + 1) % Z, req, owner)
    left = (y * Z + (z + Z - 1) % Z, req, owner)
    sibling = (patch, req, 1 - owner)
    relays = []

    def relay(block, at):
        copy = remote(lora.at[owner, block], lora.at[owner, block], send.at[at], recv.at[at], sibling)
        copy.start()
        relays.append(copy)

    relay(z, 20)
    half = Y // 2
    for step in range(Z // 2):
        forward = (z + Z - step) % Z
        backward = (z + step) % Z
        a, b = lora.at[owner, forward], lora.at[owner, backward]
        if step == Z // 2 - 1:
            a, b = lora.at[owner, forward, pl.ds(0, half)], lora.at[owner, backward, pl.ds(half, half)]
        at = 11 + 2 * step
        first = remote(a, a, send.at[at], recv.at[at], right)
        second = remote(b, b, send.at[at + 1], recv.at[at + 1], left)
        first.start()
        second.start()
        first.wait()
        second.wait()
        if step < Z // 2 - 1:
            relay((z + Z - step - 1) % Z, 21 + 2 * step)
            relay((z + step + 1) % Z, 22 + 2 * step)
        else:
            relay((z + Z // 2) % Z, 21 + 2 * step)
    for copy in relays:
        copy.wait()


def first_kernel(
    source, piece, image_adapter, bank_row, embedding, weight, gain, shift,
    top, bot, col, norm, lora,
    own, held, one, two, local_sem, edge_send, edge_recv, one_send, one_recv, two_send, two_recv, bank_send, bank_recv,
):
    fetch = pltpu.make_async_copy(source, own, local_sem)
    fetch.start()
    greet(True)
    borders = start_borders(source, top, bot, col, edge_send, edge_recv)
    fetch.wait()
    rows = own.shape[1]
    count = rows * own.shape[2]
    for image in range(2):
        mean, spread = local_stats(lambda r: own[image, r], rows)
        one[0, pl.ds(image, 1)] = mean
        one[0, pl.ds(2 + image, 1)] = spread
    one[0, pl.ds(4, 4)] = jnp.zeros((4, own.shape[3]), F32)
    copies = start_exchange(one, one_send, one_recv, first_peers())
    u = embedding[...].astype(F32)
    temb = (u / (1.0 + jnp.exp(-u))).astype(BF16)
    norm[pl.ds(5, 2)] = jnp.dot(temb, weight[...], preferred_element_type=F32)
    norm[pl.ds(7, 1)] = jnp.zeros((1, own.shape[3]), F32)
    for copy in copies:
        copy.wait()
    mean, spread = combine(one, float(count))
    two[0, pl.ds(0, 2)] = mean
    two[0, pl.ds(2, 2)] = spread
    two[0, pl.ds(4, 4)] = jnp.zeros((4, own.shape[3]), F32)
    copies = start_exchange(two, two_send, two_recv, second_peers())
    for copy in copies:
        copy.wait()
    mean, spread = combine(two, float(count * 2 * Y))
    center, scale, offset = finish_norm(
        mean, spread, float(count * 2 * Y * Z), gain[pl.ds(0, 1)], shift[pl.ds(0, 1)]
    )
    norm[pl.ds(0, 2)] = center
    norm[pl.ds(2, 2)] = scale
    norm[pl.ds(4, 1)] = offset
    gather_bank(piece, image_adapter, bank_row, held, lora, bank_send, bank_recv)
    wait_borders(borders)


def second_kernel(
    source, stats, gain, shift,
    top, bot, col, norm,
    one, two, edge_send, edge_recv, one_send, one_recv, two_send, two_recv,
):
    greet(False)
    borders = start_borders(source, top, bot, col, edge_send, edge_recv)
    count = source.shape[1] * source.shape[2]
    one[0] = stats[...]
    copies = start_exchange(one, one_send, one_recv, first_peers())
    norm[pl.ds(5, 3)] = jnp.zeros((3, stats.shape[1]), F32)
    for copy in copies:
        copy.wait()
    mean, spread = combine(one, float(count))
    two[0, pl.ds(0, 2)] = mean
    two[0, pl.ds(2, 2)] = spread
    two[0, pl.ds(4, 4)] = jnp.zeros((4, stats.shape[1]), F32)
    copies = start_exchange(two, two_send, two_recv, second_peers())
    for copy in copies:
        copy.wait()
    mean, spread = combine(two, float(count * 2 * Y))
    center, scale, offset = finish_norm(
        mean, spread, float(count * 2 * Y * Z), gain[pl.ds(1, 1)], shift[pl.ds(1, 1)]
    )
    norm[pl.ds(0, 2)] = center
    norm[pl.ds(2, 2)] = scale
    norm[pl.ds(4, 1)] = offset
    wait_borders(borders)


def conv_kernel(which, source, top, bot, col, norm, kernel, lora, *rest):
    if which == 0:
        out, stats, wide, tail, flat, expand, total, rem = rest
    else:
        latents, out, wide, tail, flat, expand, total, rem = rest
    patch, req, owner, y, z = place()
    rows, columns, chans = source.shape[1:]
    pieces = Y * Z
    piece_rows = 9 * chans // pieces
    up_at = -(-piece_rows // 16) * 16
    main = 256
    lane = lax.broadcasted_iota(jnp.int32, (3 * chans, 128), 1)
    index = lax.broadcasted_iota(jnp.int32, (columns, 1), 0)
    across = lax.broadcasted_iota(jnp.int32, (rows + 2, 1), 0)
    beyond = ((patch > 0) | (across > 0)) & ((patch < pieces - 1) | (across < rows + 1))

    def per_image(image, carry):
        for p in range(pieces):
            flat[pl.ds(p * piece_rows, piece_rows)] = lora[image, p % Z, p // Z, pl.ds(0, piece_rows)].astype(F32)
        for row_off in range(3):
            down = flat[pl.ds(row_off * 3 * chans, 3 * chans)]
            if which == 1:
                down = pltpu.roll(down, 64, 1)
            base = kernel[row_off, :, pl.ds(main, chans - main)].astype(F32)
            base = jnp.concatenate([base, jnp.zeros_like(base)], axis=1)
            tail[row_off] = jnp.where(lane >= 64, down, base).astype(BF16)
        ups = jnp.concatenate(
            [lora[image, p % Z, p // Z, pl.ds(up_at, 16)] for p in range(pieces)], axis=0
        )
        q = lax.broadcasted_iota(jnp.int32, (128, pieces * 16), 0) - 64
        s = lax.broadcasted_iota(jnp.int32, (128, pieces * 16), 1)
        for b in range(3):
            hit = (q >= 0) & (s == (q >> 1) * 16 + 4 * b + 2 * which + (q & 1))
            pick = jnp.where(hit, 1.0, 0.0).astype(BF16)
            expand[:, pl.ds(b * 128, 128)] = jnp.dot(pick, ups, preferred_element_type=F32).astype(BF16)

        center = norm[pl.ds(image, 1)]
        scale = norm[pl.ds(2 + image, 1)]
        offset = norm[pl.ds(4, 1)]

        def activate(x):
            h = (x.astype(F32) - center) * scale + offset
            return h + h * jnp.tanh(h)

        border = jnp.where(owner == 0, col[image, :, 0, :].astype(F32), col[image, :, EDGE - 1, :].astype(F32))
        rem[pl.ds(0, rows + 2)] = jnp.where(beyond, activate(border), 0.0)

        def widen(r, act):
            edge = rem[pl.ds(r, 1)]
            left = jnp.where(index == 0, jnp.where(owner == 1, edge, 0.0), pltpu.roll(act, 1, 0))
            right = jnp.where(
                index == columns - 1, jnp.where(owner == 0, edge, 0.0), pltpu.roll(act, columns - 1, 0)
            )
            wide[r] = jnp.concatenate([left, act, right], axis=1).astype(BF16)

        widen(0, jnp.where(patch > 0, activate(top[image]), 0.0))
        widen(rows + 1, jnp.where(patch < pieces - 1, activate(bot[image]), 0.0))

        def row(r, carry):
            widen(r + 1, activate(source[image, r]))
            return carry

        lax.fori_loop(0, rows, row, 0)

        part = rows // 2
        size = part * columns

        def chunk(c, carry):
            at = c * part
            window = [wide[pl.ds(at + d, part)].reshape(size, 3 * chans) for d in range(3)]
            last = sum(jnp.dot(window[d], tail[d], preferred_element_type=F32) for d in range(3))
            low = jnp.dot(last.astype(BF16), expand[...], preferred_element_type=F32)
            body = sum(
                jnp.dot(window[d], kernel[d, :, pl.ds(0, main)], preferred_element_type=F32) for d in range(3)
            )
            total[:, pl.ds(0, main)] = body + low[:, 0:main]
            total[:, pl.ds(main, 128)] = last + low[:, main:]
            for r in range(part):
                value = total[pl.ds(r * columns, columns), pl.ds(0, chans)]
                if which == 0:
                    value = value + norm[pl.ds(5 + image, 1)]
                else:
                    value = value + latents[image, at + r].astype(F32)
                out[image, at + r] = value.astype(BF16)
            return carry

        lax.fori_loop(0, 2, chunk, 0)
        if which == 0:
            mean, spread = local_stats(lambda r: out[image, r], rows)
            stats[pl.ds(image, 1)] = mean
            stats[pl.ds(2 + image, 1)] = spread
        return carry

    lax.fori_loop(0, 2, per_image, 0)
    if which == 0:
        stats[pl.ds(4, 4)] = jnp.zeros((4, chans), F32)


VM = pl.BlockSpec(memory_space=pltpu.VMEM)
HB = pl.BlockSpec(memory_space=pl.ANY)
SM = pl.BlockSpec(memory_space=pltpu.SMEM)
DMA = pltpu.SemaphoreType.DMA


def border_shapes(images, rows, columns, chans):
    line = jax.ShapeDtypeStruct((images, columns, chans), BF16)
    return [
        line,
        line,
        jax.ShapeDtypeStruct((images, rows + 2, EDGE, chans), BF16),
        jax.ShapeDtypeStruct((8, chans), F32),
    ]


def local(
    latents, timestep_embedding, embedding_weight, gain, shift, kernel_weight, reduce_library, expand_library,
    image_adapter, adapter_bank_row,
):
    images, rows, columns, chans = latents.shape
    pieces = Y * Z
    piece_rows = 9 * chans // pieces
    up_at = -(-piece_rows // 16) * 16
    down = reduce_library[0].reshape(2, piece_rows, RANK)
    down = jnp.concatenate([down[1], down[0]], axis=1)
    up = jnp.pad(expand_library[0].reshape(4, chans), ((0, 0), (0, 64))).reshape(4, 3, 128)
    up = jnp.swapaxes(up, 0, 1).reshape(12, 128)
    piece = jnp.concatenate(
        [jnp.pad(down, ((0, up_at - piece_rows), (0, 0))), jnp.pad(up, ((0, 4), (0, 0)))], axis=0
    )
    deep = up_at + 16
    exchange = [
        pltpu.VMEM((2 * Y, 8, chans), F32),
        pltpu.VMEM((Z, 8, chans), F32),
    ]
    exchange_sems = [DMA((5,)), DMA((5,)), DMA((2 * Y,)), DMA((2 * Y,)), DMA((Z,)), DMA((Z,))]
    top, bot, col, norm, lora = pl.pallas_call(
        first_kernel,
        out_shape=border_shapes(images, rows, columns, chans)
        + [jax.ShapeDtypeStruct((2, Z, Y, deep, 128), BF16)],
        in_specs=[HB, VM, SM, SM, VM, VM, VM, VM],
        out_specs=[VM] * 5,
        scratch_shapes=[
            pltpu.VMEM((images, rows, columns, chans), BF16),
            pltpu.VMEM((8, deep, 128), BF16),
            *exchange,
            DMA,
            *exchange_sems,
            DMA((32,)),
            DMA((32,)),
        ],
        compiler_params=pltpu.CompilerParams(
            collective_id=0, has_side_effects=True, vmem_limit_bytes=24 * 2**20
        ),
        name="exchange_latents",
    )(latents, piece, image_adapter, adapter_bank_row, timestep_embedding, embedding_weight, gain, shift)

    weights = kernel_weight.reshape(2, 3, 3 * chans, chans)

    def conv(which, source, top, bot, col, norm, extra):
        out_shape = [jax.ShapeDtypeStruct((images, rows, columns, chans), BF16)]
        if which == 0:
            out_shape.append(jax.ShapeDtypeStruct((8, chans), F32))
        return pl.pallas_call(
            functools.partial(conv_kernel, which),
            out_shape=out_shape,
            grid=(1,),
            in_specs=[VM] * 5
            + [pl.BlockSpec((None, 3, 3 * chans, chans), lambda i: (which, 0, 0, 0))]
            + [VM] * (1 + len(extra)),
            out_specs=[VM] * len(out_shape),
            scratch_shapes=[
                pltpu.VMEM((rows + 2, columns, 3 * chans), BF16),
                pltpu.VMEM((3, 3 * chans, 128), BF16),
                pltpu.VMEM((9 * chans, 128), F32),
                pltpu.VMEM((128, 384), BF16),
                pltpu.VMEM((rows // 2 * columns, 384), F32),
                pltpu.VMEM((16, chans), F32),
            ],
            compiler_params=pltpu.CompilerParams(vmem_limit_bytes=50 * 2**20),
            name="conv",
        )(source, top, bot, col, norm, weights, lora, *extra)

    hidden, stats = conv(0, latents, top, bot, col, norm, ())
    top, bot, col, norm = pl.pallas_call(
        second_kernel,
        out_shape=border_shapes(images, rows, columns, chans),
        in_specs=[HB, VM, VM, VM],
        out_specs=[VM] * 4,
        scratch_shapes=[*exchange, *exchange_sems],
        compiler_params=pltpu.CompilerParams(
            collective_id=1, has_side_effects=True, vmem_limit_bytes=24 * 2**20
        ),
        name="exchange_hidden",
    )(hidden, stats, gain, shift)
    (result,) = conv(1, hidden, top, bot, col, norm, (latents,))
    return result


def solution(mesh):
    in_specs = (
        P("req", "patch", "owner", None),
        P("req", None),
        P(),
        P(),
        P(),
        P(),
        P(("req", "owner"), None, "patch"),
        P(("req", "owner"), None, "patch"),
        P("req", None),
        P(),
    )
    return jax.shard_map(
        local, mesh=mesh, in_specs=in_specs, out_specs=P("req", "patch", "owner", None), check_vma=False
    )
```

time: 784 us -> 120 us (0.15)
  blocking collectives: 614 us -> 0 us
  Pallas kernels: 0 us -> 111 us
  matrix products: 79 us -> 0 us
  local copies, waits for them, and re-layouts: 37.7 us -> 8.92 us
  other arithmetic: 17 us -> 0.1 us
  starting transfers between devices: 15 us -> 0 us
  between operations: 14.1 us -> 0.14 us
    psum x4 -> x0, blocking collectives: 510 us -> none  [the longest x2 258 us: group_act(): total = lax.psum(jnp.sum(grouped, axis=(1, 2, 4)), ('patch', 'owner'))]
    pallas_call x0 -> x4, Pallas kernels: none -> 111 us  [the longest x1 53 us: local(): pl.pallas_call(first_kernel, out_shape=border_shapes(images, rows, column...]
    all_gather x3 -> x0, blocking collectives: 104 us -> none  [the longest x1 47.2 us: local(): lax.all_gather(plugin_reduce_library, 'patch', axis=2, tiled=True)]
    dot_general x23 -> x0, matrix products: 79 us -> none  [the longest x18 62.9 us: block_conv(): jnp.einsum('bhwc,bcd->bhwd', window, joined[:, tap], preferred_element_ty...]
    ppermute x8 -> x0, starting transfers between devices: 15 us -> none  [the longest x4 9.78 us: padded_2(): lax.ppermute(lax.slice_in_dim(block, 0, width, axis=dim), axis, backward)]
    slice x10 -> x1, local copies, waits for them, and re-layouts: 15.8 us -> 0.94 us  [local(): down = jnp.concatenate([down[1], down[0]], axis=1)]
    concatenate x4 -> x2, other arithmetic: 11.1 us -> 0.1 us  [the longest x1 0.09 us: local(): down = jnp.concatenate([down[1], down[0]], axis=1)]
  transfers between devices with their start and end apart: 9 -> 0, of which waited for: 1 -> 0; matrix products, arithmetic and copies ran while one was open for 5% -> 0% of each run, Pallas kernels for 0% -> 0%
where the time goes in v1:
time: 120 us
  Pallas kernels  111 us (92%)
  local copies, waits for them, and re-layouts  8.92 us (7%)
    pallas_call x1, Pallas kernels, local(): pl.pallas_call(first_kernel, out_shape=border_shapes(images, rows, column...  53 us
    pallas_call x2, Pallas kernels, conv(): pl.pallas_call(functools.partial(conv_kernel, which), out_shape=out_shape...  42.2 us
    pallas_call x1, Pallas kernels, local(): pl.pallas_call(second_kernel, out_shape=border_shapes(images, rows, colum...  15.8 us
    unnamed x15, local copies, waits for them, and re-layouts  5.43 us

profile of v1, /device:TPU:1, one launch (start us, length us, event | category | flops | bytes accessed | tf_op | source)
XLA Modules:
  0.0 120.2 jit_solution(1427722033658650858)
XLA Ops:
  0.0 0.7 copy.18.image_adapter
  0.7 0.8 reshape_squeeze.4
  1.5 0.9 slice_reduce_fusion.1
  2.5 0.1 squeeze.6
  2.6 0.1 squeeze.7
  2.7 0.1 fusion.4
  2.8 1.5 %copy.19.weight = bf16[1280,320]{1,0:T(8,128)(2,1)S(1)} copy(bf16[1280,320]{0,1:T(8,128)(2,1)} %param.12) | data formatting | bytes 1638400 | tf_op args[2]
  4.3 0.0 copy-start.2
  4.3 0.0 copy-start.3
  4.3 0.0 copy-start.4
  4.3 0.0 copy-start.5
  4.4 1.9 %copy.20.source.rest_0_ = bf16[2,8,128,320]{3,2,1,0:T(8,128)(2,1)S(1)} copy(bf16[2,8,128,320]{2,3,1,0:T(8,128)(2,1)} %param.10) | data formatting | bytes 2621440 | tf_op args[0]
  6.2 0.0 copy-done.2
  6.2 0.0 copy-done.3
  6.3 0.0 copy-done.4
  6.3 0.0 copy-done.5
  6.3 0.0 copy-start
  6.3 53.0 %exchange_latents.1 = (bf16[2,128,320]{2,1,0:T(8,128)(2,1)S(1)}, bf16[2,128,320]{2,1,0:T(8,128)(2,1)S(1)}, bf16[2,10,16,320]{3,2,1,0:T(8,128)(2,1)S(1)}, f32[8,3...) custom-call(bf16[2,8,128,320]{3,2,1,0:T(8,128)(2,1)S(1)} %copy.20.source.rest_0_, bf16[112,128]{1,0:T(8,128)(2,1)S(1)} %fusion.3.piece, ...), custom_call_target="tpu_custom_call" | custom-call | tf_op jit(solution)/shard_map/exchange_latents/pallas_call | solution.py:451
  59.3 0.0 copy-start.1
  59.3 1.2 %copy-done.1 = bf16[2,8,4,112,128]{4,3,2,1,0:T(8,128)(2,1)} copy-done((bf16[2,8,4,112,128]{4,3,2,1,0:T(8,128)(2,1)}, bf16[2,8,4,112,128]{4,3,2,1,0:T(8,128)(2,1)S(1)}, u32[]{:S(2)}) %copy-start.1) | copy-done | bytes 1835032
  60.5 21.4 %conv.2 = (bf16[2,8,128,320]{3,2,1,0:T(8,128)(2,1)S(1)}, f32[8,320]{1,0:T(8,128)S(1)}) custom-call(bf16[2,8,128,320]{3,2,1,0:T(8,128)(2,1)S(1)} %copy.20.source.rest_0_, bf16[2,128,320]{2,1,0:T(8,128)(2,1)S(1)} %get-tuple-element.16.top, bf16[2,128,320]{2,1,0:T(8,128)(2,1)S(1)} %get-tuple-element.17.bot, bf16[2,10,16,320]{3,2,1,0:T(8,128)(2,1)S(1)} %get-tuple-element.18.col, ...), custom_call_target="tpu_custom_call" | custom-call | tf_op jit(solution)/shard_map/conv/pallas_call | solution.py:478
  81.9 15.8 %exchange_hidden.1 = (bf16[2,128,320]{2,1,0:T(8,128)(2,1)S(1)}, bf16[2,128,320]{2,1,0:T(8,128)(2,1)S(1)}, bf16[2,10,16,320]{3,2,1,0:T(8,128)(2,1)S(1)}, f32[8,320]{1,0:T(8,128)S(1)}) custom-call(bf16[2,8,128,320]{3,2,1,0:T(8,128)(2,1)S(1)} %get-tuple-element.21.source, f32[8,320]{1,0:T(8,128)S(1)} %get-tuple-element.22.stats, f32[2,320]{1,0:T(2,128)S(1)} %copy-done.2, ...), custom_call_target="tpu_custom_call" | custom-call | tf_op jit(solution)/shard_map/exchange_hidden/pallas_call | solution.py:499
  97.7 20.9 %conv.3 = bf16[2,8,128,320]{3,2,1,0:T(8,128)(2,1)S(1)} custom-call(bf16[2,8,128,320]{3,2,1,0:T(8,128)(2,1)S(1)} %get-tuple-element.21.source, bf16[2,128,320]{2,1,0:T(8,128)(2,1)S(1)} %get-tuple-element.23.top, bf16[2,128,320]{2,1,0:T(8,128)(2,1)S(1)} %get-tuple-element.24.bot, bf16[2,10,16,320]{3,2,1,0:T(8,128)(2,1)S(1)} %get-tuple-element.25.col, ...), custom_call_target="tpu_custom_call" | custom-call | tf_op jit(solution)/shard_map/conv/pallas_call | solution.py:478
  118.6 1.6 %copy.22 = bf16[2,8,128,320]{2,3,1,0:T(8,128)(2,1)} copy(bf16[2,8,128,320]{3,2,1,0:T(8,128)(2,1)S(1)} %conv.3) | data formatting | bytes 2621440 | tf_op jit(solution)/shard_map/conv/pallas_call | solution.py:478
  (4 shorter events, 0.0 us)
Async XLA Ops:
  4.3 1.9 %copy-start.2 = (f32[2,320]{1,0:T(2,128)S(1)}, f32[2,320]{1,0:T(2,128)}, u32[]{:S(2)}) copy-start(f32[2,320]{1,0:T(2,128)} %gain.3) | copy-start | bytes 7684
  4.3 1.9 %copy-start.3 = (f32[2,320]{1,0:T(2,128)S(1)}, f32[2,320]{1,0:T(2,128)}, u32[]{:S(2)}) copy-start(f32[2,320]{1,0:T(2,128)} %shift.3) | copy-start | bytes 7684
  4.3 1.9 %copy-start.4 = (bf16[2,1280]{1,0:T(2,128)(2,1)S(1)}, bf16[2,1280]{1,0:T(2,128)(2,1)}, u32[]{:S(2)}) copy-start(bf16[2,1280]{1,0:T(2,128)(2,1)} %embedding.1) | copy-start | bytes 15364
  4.3 1.9 %copy-start.5 = (s32[8]{0:T(128)S(1)}, s32[8]{0:T(128)}, u32[]{:S(2)}) copy-start(s32[8]{0:T(128)} %bank_row.1) | copy-start | bytes 100
  6.3 75.6 %copy-start = (bf16[2,8,128,320]{3,2,1,0:T(8,128)(2,1)}, bf16[2,8,128,320]{3,2,1,0:T(8,128)(2,1)S(1)}, u32[]{:S(2)}) copy-start(bf16[2,8,128,320]{3,2,1,0:T(8,128)(2,1)S(1)} %copy.20.source.rest_0_) | copy-start | bytes 3932164
  59.3 1.3 %copy-start.1 = (bf16[2,8,4,112,128]{4,3,2,1,0:T(8,128)(2,1)}, bf16[2,8,4,112,128]{4,3,2,1,0:T(8,128)(2,1)S(1)}, u32[]{:S(2)}) copy-start(bf16[2,8,4,112,128]{4,3,2,1,0:T(8,128)(2,1)S(1)} %get-tuple-element.20.lora) | copy-start | bytes 5505028

commit v2 on v0

v2 whole, which is shorter than its diff:
```python
import jax
import jax.numpy as jnp
from jax import lax
from jax.experimental import pallas as pl
from jax.experimental.pallas import tpu as pltpu
from jax.sharding import PartitionSpec as P

MESH = pl.DeviceIdType.MESH
F32, BF16 = jnp.float32, jnp.bfloat16
Y, Z = 4, 8
RANK = 64
EDGE = 16
GROUP = 10


def remote(src, dst, send, recv, device):
    return pltpu.make_async_remote_copy(
        src_ref=src, dst_ref=dst, send_sem=send, recv_sem=recv, device_id=device, device_id_type=MESH
    )


def place():
    patch, req, owner = lax.axis_index("patch"), lax.axis_index("req"), lax.axis_index("owner")
    return patch, req, owner, patch // Z, patch % Z


def greet():
    patch, req, owner, y, z = place()
    sem = pltpu.get_barrier_semaphore()
    count = 0

    def signal(device):
        pl.semaphore_signal(sem, inc=1, device_id=device, device_id_type=MESH)

    for k in range(1, Y * Z):
        signal(((patch + k) % (Y * Z), req, owner))
        count += 1
    for k in range(1, 2 * Y, 2):
        g = (y * 2 + owner + k) % (2 * Y)
        signal(((g // 2) * Z + z, req, g % 2))
        count += 1
    for step in (1, Y * Z - 1):
        signal(((patch + step) % (Y * Z), req, 1 - owner))
        count += 1
    for k in range(1, 8):
        g = (req * 2 + owner + k) % 8
        signal((patch, g // 2, g % 2))
        count += 1
    return lambda: pl.semaphore_wait(sem, count)


def start_borders(src, top, bot, col, image, send, recv):
    patch, req, owner, y, z = place()
    rows = src.shape[1]
    last = Y * Z - 1
    edge = pl.multiple_of((1 - owner) * (src.shape[2] - EDGE), EDGE)
    cols = pl.ds(edge, EDGE)

    def copy(at, block, target, device):
        return remote(block, target, send.at[image, at], recv.at[image, at], device)

    down, up = patch < last, patch > 0
    copies = [
        (down, up, copy(0, src.at[image, rows - 1], top.at[image], (patch + 1, req, owner))),
        (up, down, copy(1, src.at[image, 0], bot.at[image], (patch - 1, req, owner))),
        (down, up, copy(2, src.at[image, rows - 1, cols], col.at[image, 0], (patch + 1, req, 1 - owner))),
        (up, down, copy(3, src.at[image, 0, cols], col.at[image, rows + 1], (patch - 1, req, 1 - owner))),
        (None, None, copy(4, src.at[image, :, cols], col.at[image, pl.ds(1, rows)], (patch, req, 1 - owner))),
    ]
    for sends, _, item in copies:
        if sends is None:
            item.start()
        else:
            pl.when(sends)(item.start)
    return copies


def clear_borders(top, bot, col):
    patch = lax.axis_index("patch")
    end = col.shape[1] - 1

    @pl.when(patch == 0)
    def _():
        top[...] = jnp.zeros_like(top)
        col[:, 0] = jnp.zeros_like(col[:, 0])

    @pl.when(patch == Y * Z - 1)
    def _():
        bot[...] = jnp.zeros_like(bot)
        col[:, end] = jnp.zeros_like(col[:, end])


def wait_borders(copies):
    for sends, receives, copy in copies:
        if sends is None:
            copy.wait_send()
            copy.wait_recv()
        else:
            pl.when(sends)(copy.wait_send)
            pl.when(receives)(copy.wait_recv)


def local_stats(rows_of, rows):
    def add(f):
        def step(r, total):
            x = f(rows_of(r).astype(F32))
            return total + jnp.sum(x.reshape(x.shape[0] // 8, 8, x.shape[1]), axis=0)

        return step

    chans = rows_of(0).shape[1]
    count = rows * rows_of(0).shape[0]
    zero = jnp.zeros((8, chans), F32)
    total = lax.fori_loop(0, rows, add(lambda x: x), zero)
    mean = jnp.sum(total, axis=0, keepdims=True) * (1.0 / count)
    spread = lax.fori_loop(0, rows, add(lambda x: (x - mean) * (x - mean)), zero)
    return mean, jnp.sum(spread, axis=0, keepdims=True)


def start_exchange(slots, send, recv, peers):
    copies = [
        remote(slots.at[0], slots.at[k], send.at[k], recv.at[k], peer) for k, peer in enumerate(peers, 1)
    ]
    for copy in copies:
        copy.start()
    return copies


def combine(slots, count):
    values = slots[...]
    total = jnp.sum(values, axis=0)
    mean = total * (1.0 / values.shape[0])
    off = values - mean[None]
    between = jnp.sum(off * off, axis=0)
    return mean[0:2], total[2:4] + count * between[0:2]


def first_peers():
    patch, req, owner, y, z = place()
    peers = []
    for k in range(1, 2 * Y):
        g = (y * 2 + owner + k) % (2 * Y)
        peers.append(((g // 2) * Z + z, req, g % 2))
    return peers


def second_peers():
    patch, req, owner, y, z = place()
    return [(y * Z + (z + k) % Z, req, owner) for k in range(1, Z)]


def group_mean(values, groups):
    high = values.astype(BF16)
    rest = values - high.astype(F32)
    middle = rest.astype(BF16)
    low = (rest - middle.astype(F32)).astype(BF16)
    total = (
        jnp.dot(high, groups, preferred_element_type=F32)
        + jnp.dot(middle, groups, preferred_element_type=F32)
        + jnp.dot(low, groups, preferred_element_type=F32)
    )
    return total * (1.0 / GROUP)


def finish_norm(mean, spread, count, gain, shift):
    chans = mean.shape[1]
    row = lax.broadcasted_iota(jnp.int32, (chans, chans), 0)
    column = lax.broadcasted_iota(jnp.int32, (chans, chans), 1)
    groups = jnp.where((row * 6554) >> 16 == (column * 6554) >> 16, 1.0, 0.0).astype(BF16)
    both = jnp.concatenate([mean, mean, mean, mean], axis=0)
    center = group_mean(both, groups)[0:2]
    off = mean - center
    local = spread * (1.0 / count) + off * off
    var = group_mean(jnp.concatenate([local, local, local, local], axis=0), groups)[0:2]
    scale = gain / jnp.sqrt(var + 1e-05)
    return center, 0.5 * scale, 0.5 * shift


def lay_piece(reduce_row, expand_row, piece):
    down = reduce_row[0].astype(F32)
    up = expand_row[0].astype(F32)
    piece[...] = jnp.zeros_like(piece)
    for i in range(down.shape[1] // 128):
        piece[:, i, :] = down[:, i * 128 : i * 128 + 128]
    for i in range(up.shape[1] // 128):
        piece[:, UP_AT + i, :] = up[:, i * 128 : i * 128 + 128]
    return piece[...].astype(BF16)


def send_pieces(lora, send, recv):
    patch, req, owner, y, z = place()
    copies = []
    for k in range(1, Y * Z):
        block = lora.at[owner, patch]
        copy = remote(block, block, send.at[k], recv.at[k], ((patch + k) % (Y * Z), req, owner))
        copy.start()
        copies.append(copy)
    return copies


def lay_adapter(lora, image, base, tail, expand, flat, ups, wide_up):
    pieces = Y * Z
    depth = tail.shape[1] * 3 // pieces
    half = depth // 2

    def lay(p, carry):
        value = lora[image, p].astype(F32)
        down = value[0:half]
        flat[pl.ds(p * depth, half, 2)] = pltpu.roll(down, 64, 1)
        flat[pl.ds(p * depth + 1, half, 2)] = down
        ups[pl.ds(pl.multiple_of(p * 8, 8), 8)] = value[UP_AT : UP_AT + 8]
        return carry

    lax.fori_loop(0, pieces, lay, 0)
    lane = lax.broadcasted_iota(jnp.int32, base.shape[1:], 1)
    for d in range(3):
        down = flat[pl.ds(d * base.shape[1], base.shape[1])]
        tail[d] = jnp.where(lane >= 64, down, base[d].astype(F32)).astype(BF16)
    line = [ups[pl.ds(k, pieces, 8)] for k in range(5)]
    turned = [pltpu.roll(v, 64, 1) for v in line]
    low = lax.broadcasted_iota(jnp.int32, line[0].shape, 1) < 64
    even = line[0:3]
    odd = [jnp.where(low, turned[2], turned[3]), jnp.where(low, turned[3], turned[4]), turned[4]]
    for b in range(3):
        wide_up[pl.ds(0, 64)] = jnp.zeros((64, 128), F32)
        wide_up[pl.ds(64, pieces, 2)] = even[b]
        wide_up[pl.ds(65, pieces, 2)] = odd[b]
        expand[:, pl.ds(b * 128, 128)] = wide_up[...].astype(BF16)


def widen_image(source, top, bot, col, norm, image, wide, rem):
    patch, req, owner, y, z = place()
    rows, columns = source.shape[1:3]
    last = Y * Z - 1
    index = lax.broadcasted_iota(jnp.int32, (columns, 1), 0)
    across = lax.broadcasted_iota(jnp.int32, (rows + 2, 1), 0)
    beyond = ((patch > 0) | (across > 0)) & ((patch < last) | (across < rows + 1))
    center = norm[pl.ds(image, 1)]
    scale = norm[pl.ds(2 + image, 1)]
    offset = norm[pl.ds(4, 1)]

    def activate(x):
        h = (x.astype(F32) - center) * scale + offset
        return h + h * jnp.tanh(h)

    border = jnp.where(owner == 0, col[image, :, 0, :].astype(F32), col[image, :, EDGE - 1, :].astype(F32))
    rem[pl.ds(0, rows + 2)] = jnp.where(beyond, activate(border), 0.0)

    def lay(r, act):
        edge = rem[pl.ds(r, 1)]
        left = jnp.where(index == 0, jnp.where(owner == 1, edge, 0.0), pltpu.roll(act, 1, 0))
        right = jnp.where(
            index == columns - 1, jnp.where(owner == 0, edge, 0.0), pltpu.roll(act, columns - 1, 0)
        )
        wide[image, r] = jnp.concatenate([left, act, right], axis=1).astype(BF16)

    lay(0, jnp.where(patch > 0, activate(top[image]), 0.0))
    lay(rows + 1, jnp.where(patch < last, activate(bot[image]), 0.0))

    def row(r, carry):
        lay(r + 1, activate(source[image, r]))
        return carry

    lax.fori_loop(0, rows, row, 0)


def windows(wide, image, at, part):
    columns, depth = wide.shape[2:]
    return [wide[image, pl.ds(at + d, part)].reshape(part * columns, depth) for d in range(3)]


def dots(window, matrix, lanes):
    return sum(jnp.dot(window[d], matrix[d, :, lanes], preferred_element_type=F32) for d in range(3))


MAIN, REST = pl.ds(0, 256), pl.ds(256, 128)
UP_AT = 48


def block_kernel(
    raw, reduce_row, expand_row, image_adapter, bank_row, embedding, weight, gain, shift, kernels_hbm,
    out,
    raw_own, own, hidden, kernels, wide, total, base, tail, expand, flat, ups, wide_up, rem,
    piece, held, lora, top, bot, col, top2, bot2, col2, norm, one, two, one2, two2,
    local_sem, bank_send, bank_recv, lora_send, lora_recv, relay_send, relay_recv,
    edge_send, edge_recv, edge2_send, edge2_recv, x_send, x_recv,
):
    patch, req, owner, y, z = place()
    images, rows, columns, chans = own.shape
    count = rows * columns
    fetch = pltpu.make_async_copy(raw, raw_own, local_sem.at[0])
    fetch.start()
    fetch_kernels = pltpu.make_async_copy(kernels_hbm, kernels, local_sem.at[1])
    fetch_kernels.start()
    arrived = greet()
    me = req * 2 + owner
    held[me] = lay_piece(reduce_row, expand_row, piece)
    clear_borders(top, bot, col)
    clear_borders(top2, bot2, col2)
    for block in (one, two, one2, two2):
        block[0, pl.ds(4, 4)] = jnp.zeros((4, chans), F32)
    fetch.wait()

    def turn(t, carry):
        image, r = t // rows, t % rows
        own[image, r] = jnp.transpose(raw_own[image, r].astype(F32)).astype(BF16)
        return carry

    lax.fori_loop(0, images * rows, turn, 0)

    def stats(source, image, target):
        mean, spread = local_stats(lambda r: source[image, r], rows)
        target[0, pl.ds(image, 1)] = mean
        target[0, pl.ds(2 + image, 1)] = spread

    for image in range(images):
        stats(own, image, one)
    arrived()

    first = start_exchange(one, x_send.at[0], x_recv.at[0], first_peers())
    bank = []
    for k in range(1, 8):
        g = (me + k) % 8
        copy = remote(held.at[me], held.at[me], bank_send.at[k], bank_recv.at[k], (patch, g // 2, g % 2))
        copy.start()
        bank.append(copy)
    borders = [start_borders(own, top, bot, col, i, edge_send, edge_recv) for i in range(images)]

    u = embedding[...].astype(F32)
    temb = (u / (1.0 + jnp.exp(-u))).astype(BF16)
    proj = lax.dot_general(temb, weight[...], (((1,), (1,)), ((), ())), preferred_element_type=F32)
    norm[0, pl.ds(5, 2)] = proj
    fetch_kernels.wait()

    def middle(first, one, two, send, recv):
        for copy in first:
            copy.wait()
        mean, spread = combine(one, float(count))
        two[0, pl.ds(0, 2)] = mean
        two[0, pl.ds(2, 2)] = spread
        return start_exchange(two, send, recv, second_peers())

    def finish(second, two, which):
        for copy in second:
            copy.wait()
        mean, spread = combine(two, float(count * 2 * Y))
        center, scale, offset = finish_norm(
            mean, spread, float(count * 2 * Y * Z), gain[pl.ds(which, 1)], shift[pl.ds(which, 1)]
        )
        norm[which, pl.ds(0, 2)] = center
        norm[which, pl.ds(2, 2)] = scale
        norm[which, pl.ds(4, 1)] = offset

    second = middle(first, one, two, x_send.at[1], x_recv.at[1])
    for copy in bank:
        copy.wait()
    chosen = held[bank_row[image_adapter[0, owner]]]
    lora[0, owner, patch] = chosen[0]
    lora[1, owner, patch] = chosen[1]
    pieces = [send_pieces(lora.at[0], lora_send.at[0], lora_recv.at[0])]
    for which in range(2):
        for d in range(3):
            last = kernels[which, d, :, pl.ds(256, chans - 256)].astype(F32)
            base[which, d] = jnp.concatenate([last, jnp.zeros_like(last)], axis=1).astype(BF16)
    finish(second, two, 0)
    for copies in borders:
        wait_borders(copies)

    part = rows // 2
    size = part * columns
    order = (owner, 1 - owner)

    def main_dots(image):
        def chunk(c, carry):
            window = windows(wide, image, c * part, part)
            total[image, pl.ds(pl.multiple_of(c * size, size), size), MAIN] = dots(window, kernels.at[0], MAIN)
            return carry

        lax.fori_loop(0, 2, chunk, 0)

    for step, image in enumerate(order):
        widen_image(own, top, bot, col, norm.at[0], image, wide, rem)
        main_dots(image)
        if step == 0:
            pieces.append(send_pieces(lora.at[1], lora_send.at[1], lora_recv.at[1]))

    def adapter(which, step, relay):
        if step == 0:
            for copy in pieces[which]:
                copy.wait()
            block = lora.at[which, owner]
            relay = remote(block, block, relay_send.at[which], relay_recv.at[which], (patch, req, 1 - owner))
            relay.start()
        else:
            relay.wait()
        image = order[step]
        lay_adapter(
            lora.at[which], image, base.at[which], tail.at[image], expand.at[image], flat, ups, wide_up
        )
        return relay

    borders, relay = [], None
    for step, image in enumerate(order):
        relay = adapter(0, step, relay)

        def chunk(c, carry, image=image):
            at = c * part
            window = windows(wide, image, at, part)
            span = pl.ds(pl.multiple_of(c * size, size), size)
            last = dots(window, tail.at[image], pl.ds(0, 128))
            small = last.astype(BF16)
            total[image, span, REST] = last + jnp.dot(small, expand[image, :, REST], preferred_element_type=F32)
            total[image, span, MAIN] += jnp.dot(small, expand[image, :, MAIN], preferred_element_type=F32)
            bias = norm[0, pl.ds(5 + image, 1)]
            for r in range(part):
                value = total[image, pl.ds(pl.multiple_of((at + r) * columns, columns), columns), pl.ds(0, chans)]
                hidden[image, at + r] = (value + bias).astype(BF16)
            return carry

        lax.fori_loop(0, 2, chunk, 0)
        borders.append(start_borders(hidden, top2, bot2, col2, image, edge2_send, edge2_recv))
        stats(hidden, image, one2)

    first = start_exchange(one2, x_send.at[2], x_recv.at[2], first_peers())
    relay = adapter(1, 0, None)
    second = middle(first, one2, two2, x_send.at[3], x_recv.at[3])
    adapter(1, 1, relay)
    finish(second, two2, 1)
    for copies in borders:
        wait_borders(copies)

    for image in order:
        widen_image(hidden, top2, bot2, col2, norm.at[1], image, wide, rem)

        def chunk(c, carry, image=image):
            at = c * part
            window = windows(wide, image, at, part)
            last = dots(window, tail.at[image], pl.ds(0, 128))
            small = last.astype(BF16)
            body = dots(window, kernels.at[1], MAIN)
            span = pl.ds(pl.multiple_of(c * size, size), size)
            total[image, span, MAIN] = body + jnp.dot(small, expand[image, :, MAIN], preferred_element_type=F32)
            total[image, span, REST] = last + jnp.dot(small, expand[image, :, REST], preferred_element_type=F32)
            for r in range(part):
                value = total[image, pl.ds(pl.multiple_of((at + r) * columns, columns), columns), pl.ds(0, chans)]
                out[image, at + r] = (value + own[image, at + r].astype(F32)).astype(BF16)
            return carry

        lax.fori_loop(0, 2, chunk, 0)


VM = pl.BlockSpec(memory_space=pltpu.VMEM)
HB = pl.BlockSpec(memory_space=pl.ANY)
SM = pl.BlockSpec(memory_space=pltpu.SMEM)
DMA = pltpu.SemaphoreType.DMA


def local(
    latents, timestep_embedding, embedding_weight, gain, shift, kernel_weight, reduce_library, expand_library,
    image_adapter, adapter_bank_row,
):
    images, rows, columns, chans = latents.shape
    pieces = Y * Z
    deep = UP_AT + 8
    map_of = (images, rows, columns, chans)
    line = pltpu.VMEM((images, columns, chans), BF16)
    edge = pltpu.VMEM((images, rows + 2, EDGE, chans), BF16)
    return pl.pallas_call(
        block_kernel,
        out_shape=jax.ShapeDtypeStruct(map_of, BF16),
        in_specs=[HB, VM, VM, SM, SM, VM, VM, VM, VM, HB],
        out_specs=VM,
        scratch_shapes=[
            pltpu.VMEM((images, rows, chans, columns), BF16),
            pltpu.VMEM(map_of, BF16),
            pltpu.VMEM(map_of, BF16),
            pltpu.VMEM((2, 3, 3 * chans, chans), BF16),
            pltpu.VMEM((images, rows + 2, columns, 3 * chans), BF16),
            pltpu.VMEM((images, rows * columns, 384), F32),
            pltpu.VMEM((2, 3, 3 * chans, 128), BF16),
            pltpu.VMEM((images, 3, 3 * chans, 128), BF16),
            pltpu.VMEM((images, 128, 384), BF16),
            pltpu.VMEM((9 * chans, 128), F32),
            pltpu.VMEM((pieces * 8, 128), F32),
            pltpu.VMEM((128, 128), F32),
            pltpu.VMEM((16, chans), F32),
            pltpu.VMEM((2, deep, 128), F32),
            pltpu.VMEM((8, 2, deep, 128), BF16),
            pltpu.VMEM((2, images, pieces, deep, 128), BF16),
            *([line, line, edge] * 2),
            pltpu.VMEM((2, 8, chans), F32),
            *([pltpu.VMEM((2 * Y, 8, chans), F32), pltpu.VMEM((Z, 8, chans), F32)] * 2),
            DMA((2,)),
            DMA((8,)),
            DMA((8,)),
            DMA((2, pieces)),
            DMA((2, pieces)),
            DMA((2,)),
            DMA((2,)),
            *([DMA((images, 5))] * 4),
            DMA((4, 8)),
            DMA((4, 8)),
        ],
        compiler_params=pltpu.CompilerParams(
            collective_id=0, has_side_effects=True, vmem_limit_bytes=56 * 2**20
        ),
        name="resnet_block",
    )(
        jnp.swapaxes(latents, 2, 3),
        reduce_library,
        expand_library,
        image_adapter.T,
        adapter_bank_row,
        timestep_embedding,
        embedding_weight.T,
        gain,
        shift,
        kernel_weight.reshape(2, 3, 3 * chans, chans),
    )


def solution(mesh):
    in_specs = (
        P("req", "patch", "owner", None),
        P("req", None),
        P(),
        P(),
        P(),
        P(),
        P(("req", "owner"), None, "patch"),
        P(("req", "owner"), None, "patch"),
        P("req", None),
        P(),
    )
    return jax.shard_map(
        local, mesh=mesh, in_specs=in_specs, out_specs=P("req", "patch", "owner", None), check_vma=False
    )
```

time: 784 us -> 74.6 us (0.10)
  blocking collectives: 614 us -> 0 us
  matrix products: 79 us -> 0 us
  Pallas kernels: 0 us -> 71.2 us
  local copies, waits for them, and re-layouts: 37.7 us -> 2.53 us
  other arithmetic: 17 us -> 0 us
  starting transfers between devices: 15 us -> 0 us
  between operations: 14.1 us -> 0.01 us
    psum x4 -> x0, blocking collectives: 510 us -> none  [the longest x2 258 us: group_act(): total = lax.psum(jnp.sum(grouped, axis=(1, 2, 4)), ('patch', 'owner'))]
    all_gather x3 -> x0, blocking collectives: 104 us -> none  [the longest x1 47.2 us: local(): lax.all_gather(plugin_reduce_library, 'patch', axis=2, tiled=True)]
    dot_general x23 -> x0, matrix products: 79 us -> none  [the longest x18 62.9 us: block_conv(): jnp.einsum('bhwc,bcd->bhwd', window, joined[:, tap], preferred_element_ty...]
    pallas_call x0 -> x1, Pallas kernels: none -> 71.2 us  [local(): pl.pallas_call(block_kernel, out_shape=jax.ShapeDtypeStruct(map_of, BF16)...]
    slice x10 -> x0, local copies, waits for them, and re-layouts: 15.8 us -> none  [the longest x4 8.7 us: padded_2(): lax.slice_in_dim(block, 0, width, axis=dim)]
    ppermute x8 -> x0, starting transfers between devices: 15 us -> none  [the longest x4 9.78 us: padded_2(): lax.ppermute(lax.slice_in_dim(block, 0, width, axis=dim), axis, backward)]
    concatenate x4 -> x0, other arithmetic: 11.1 us -> none  [padded_2(): block = jnp.concatenate([low, block, high], axis=dim)]
  transfers between devices with their start and end apart: 9 -> 0, of which waited for: 1 -> 0; matrix products, arithmetic and copies ran while one was open for 5% -> 0% of each run, Pallas kernels for 0% -> 0%
where the time goes in v2:
time: 74.6 us; the launch traced here: 73.8 us
  Pallas kernels  71.2 us (95%)
  local copies, waits for them, and re-layouts  2.53 us (3%)
    pallas_call x1, Pallas kernels, local(): pl.pallas_call(block_kernel, out_shape=jax.ShapeDtypeStruct(map_of, BF16)...  71.2 us
    pallas_call x1, local copies, waits for them, and re-layouts, local(): pl.pallas_call(block_kernel, out_shape=jax.ShapeDtypeStruct(map_of, BF16)...  2.53 us

profile of v2, /device:TPU:1, one launch (start us, length us, event | category | flops | bytes accessed | tf_op | source)
XLA Modules:
  0.0 73.8 jit_solution(16829002389508228995)
XLA Ops:
  0.0 71.2 %resnet_block.1 = bf16[2,8,128,320]{3,2,1,0:T(8,128)(2,1)} custom-call(bf16[2,8,320,128]{3,2,1,0:T(8,128)(2,1)} %bitcast.5, bf16[1,2,5760]{2,1,0:T(2,128)(2,1)} %reduce_row.1, bf16[1,2,640]{2,1,0:T(2,128)(2,1)} %expand_row.1, s32[1,2]{1,0:T(1,128)} %bitcast.7, s32[8]{0:T(128)} %bank_row.1, bf16[2,1280]{1,0:T(2,128)(2,1)} %embedding.1, ...), custom_call_target="tpu_custom_call" | custom-call | tf_op jit(solution)/shard_map/resnet_block/pallas_call | solution.py:468
  71.2 2.5 %copy.11 = bf16[2,8,128,320]{2,3,1,0:T(8,128)(2,1)} copy(bf16[2,8,128,320]{3,2,1,0:T(8,128)(2,1)} %resnet_block.1) | data formatting | bytes 2621440 | tf_op jit(solution)/shard_map/resnet_block/pallas_call | solution.py:468

commit v3 on v2

--- a/solution.py
+++ b/solution.py
@@ -24,6 +24,16 @@
     return patch, req, owner, patch // Z, patch % Z
 
 
+def near():
+    patch, req, owner, y, z = place()
+    return [
+        (dz, dy, ((y + dy) % Y * Z + (z + dz) % Z, req, owner))
+        for dz in (2, -2, 1, -1, 0)
+        for dy in range(Y)
+        if dz or dy
+    ]
+
+
 def greet():
     patch, req, owner, y, z = place()
     sem = pltpu.get_barrier_semaphore()
@@ -32,8 +42,11 @@
     def signal(device):
         pl.semaphore_signal(sem, inc=1, device_id=device, device_id_type=MESH)
 
-    for k in range(1, Y * Z):
-        signal(((patch + k) % (Y * Z), req, owner))
+    for _, _, device in near():
+        signal(device)
+        count += 1
+    for dz in range(3, Z - 2):
+        signal((y * Z + (z + dz) % Z, req, owner))
         count += 1
     for k in range(1, 2 * Y, 2):
         g = (y * 2 + owner + k) % (2 * Y)
@@ -128,11 +141,12 @@
 
 def combine(slots, count):
     values = slots[...]
+    half = values.shape[1] // 2
     total = jnp.sum(values, axis=0)
     mean = total * (1.0 / values.shape[0])
     off = values - mean[None]
     between = jnp.sum(off * off, axis=0)
-    return mean[0:2], total[2:4] + count * between[0:2]
+    return mean[0:half], total[half:] + count * between[0:half]
 
 
 def first_peers():
@@ -149,29 +163,27 @@
     return [(y * Z + (z + k) % Z, req, owner) for k in range(1, Z)]
 
 
-def group_mean(values, groups):
-    high = values.astype(BF16)
-    rest = values - high.astype(F32)
-    middle = rest.astype(BF16)
-    low = (rest - middle.astype(F32)).astype(BF16)
-    total = (
-        jnp.dot(high, groups, preferred_element_type=F32)
-        + jnp.dot(middle, groups, preferred_element_type=F32)
-        + jnp.dot(low, groups, preferred_element_type=F32)
-    )
-    return total * (1.0 / GROUP)
-
-
-def finish_norm(mean, spread, count, gain, shift):
-    chans = mean.shape[1]
+def group_matrix(chans):
     row = lax.broadcasted_iota(jnp.int32, (chans, chans), 0)
     column = lax.broadcasted_iota(jnp.int32, (chans, chans), 1)
-    groups = jnp.where((row * 6554) >> 16 == (column * 6554) >> 16, 1.0, 0.0).astype(BF16)
-    both = jnp.concatenate([mean, mean, mean, mean], axis=0)
-    center = group_mean(both, groups)[0:2]
+    return jnp.where((row * 6554) >> 16 == (column * 6554) >> 16, 1.0, 0.0).astype(BF16)
+
+
+def group_mean(values, groups):
+    count = values.shape[0]
+    values = jnp.concatenate([values] * (8 // count), axis=0)
+    high = values.astype(BF16).astype(F32)
+    rest = values - high
+    middle = rest.astype(BF16).astype(F32)
+    parts = jnp.concatenate([high, middle, rest - middle], axis=0).astype(BF16)
+    total = jnp.dot(parts, groups, preferred_element_type=F32)
+    return (total[0:count] + total[8 : 8 + count] + total[16 : 16 + count]) * (1.0 / GROUP)
+
+
+def finish_norm(mean, spread, count, gain, shift, groups):
+    center = group_mean(mean, groups)
     off = mean - center
-    local = spread * (1.0 / count) + off * off
-    var = group_mean(jnp.concatenate([local, local, local, local], axis=0), groups)[0:2]
+    var = group_mean(spread * (1.0 / count) + off * off, groups)
     scale = gain / jnp.sqrt(var + 1e-05)
     return center, 0.5 * scale, 0.5 * shift
 
@@ -187,15 +199,34 @@
     return piece[...].astype(BF16)
 
 
-def send_pieces(lora, send, recv):
-    patch, req, owner, y, z = place()
-    copies = []
-    for k in range(1, Y * Z):
-        block = lora.at[owner, patch]
-        copy = remote(block, block, send.at[k], recv.at[k], ((patch + k) % (Y * Z), req, owner))
+def send_near(lora, send, recv):
+    patch, req, owner, y, z = place()
+    block = lora.at[owner, z, y]
+    copies = {}
+    for k, (dz, dy, device) in enumerate(near()):
+        copies[dz, dy] = remote(block, block, send.at[k], recv.at[k], device)
+        copies[dz, dy].start()
+    return copies
+
+
+def send_far(copies, lora, send, recv):
+    patch, req, owner, y, z = place()
+    half = Y // 2
+
+    def forward(at, column, ys, dz):
+        block = lora.at[owner, column, ys]
+        copy = remote(block, block, send.at[at], recv.at[at], (y * Z + (z + dz) % Z, req, owner))
         copy.start()
-        copies.append(copy)
-    return copies
+        copies[at] = copy
+
+    for dz in (2, -2):
+        for dy in range(Y):
+            copies.pop((dz, dy)).wait()
+    below, above = (z + Z - 2) % Z, (z + 2) % Z
+    forward(20, below, pl.ds(0, Y), 1)
+    forward(21, above, pl.ds(0, Y), Z - 1)
+    forward(22, below, pl.ds(0, half), 2)
+    forward(23, above, pl.ds(half, half), Z - 2)
 
 
 def lay_adapter(lora, image, base, tail, expand, flat, ups, wide_up):
@@ -204,7 +235,7 @@
     half = depth // 2
 
     def lay(p, carry):
-        value = lora[image, p].astype(F32)
+        value = lora[image, p % Z, p // Z].astype(F32)
         down = value[0:half]
         flat[pl.ds(p * depth, half, 2)] = pltpu.roll(down, 64, 1)
         flat[pl.ds(p * depth + 1, half, 2)] = down
@@ -278,9 +309,9 @@
 
 
 def block_kernel(
-    raw, reduce_row, expand_row, image_adapter, bank_row, embedding, weight, gain, shift, kernels_hbm,
+    raw, reduce_row, expand_row, image_adapter, bank_row, embedding, weight_hbm, gain, shift, kernels_hbm,
     out,
-    raw_own, own, hidden, kernels, wide, total, base, tail, expand, flat, ups, wide_up, rem,
+    raw_own, weight, groups, own, hidden, kernels, wide, total, base, tail, expand, flat, ups, wide_up, rem,
     piece, held, lora, top, bot, col, top2, bot2, col2, norm, one, two, one2, two2,
     local_sem, bank_send, bank_recv, lora_send, lora_recv, relay_send, relay_recv,
     edge_send, edge_recv, edge2_send, edge2_recv, x_send, x_recv,
@@ -292,13 +323,14 @@
     fetch.start()
     fetch_kernels = pltpu.make_async_copy(kernels_hbm, kernels, local_sem.at[1])
     fetch_kernels.start()
+    fetch_weight = pltpu.make_async_copy(weight_hbm, weight, local_sem.at[2])
+    fetch_weight.start()
     arrived = greet()
     me = req * 2 + owner
     held[me] = lay_piece(reduce_row, expand_row, piece)
     clear_borders(top, bot, col)
     clear_borders(top2, bot2, col2)
-    for block in (one, two, one2, two2):
-        block[0, pl.ds(4, 4)] = jnp.zeros((4, chans), F32)
+    groups[...] = group_matrix(chans)
     fetch.wait()
 
     def turn(t, carry):
@@ -308,13 +340,10 @@
 
     lax.fori_loop(0, images * rows, turn, 0)
 
-    def stats(source, image, target):
-        mean, spread = local_stats(lambda r: source[image, r], rows)
-        target[0, pl.ds(image, 1)] = mean
-        target[0, pl.ds(2 + image, 1)] = spread
-
     for image in range(images):
-        stats(own, image, one)
+        mean, spread = local_stats(lambda r, image=image: own[image, r], rows)
+        one[0, pl.ds(image, 1)] = mean
+        one[0, pl.ds(2 + image, 1)] = spread
     arrived()
 
     first = start_exchange(one, x_send.at[0], x_recv.at[0], first_peers())
@@ -324,129 +353,138 @@
         copy = remote(held.at[me], held.at[me], bank_send.at[k], bank_recv.at[k], (patch, g // 2, g % 2))
         copy.start()
         bank.append(copy)
-    borders = [start_borders(own, top, bot, col, i, edge_send, edge_recv) for i in range(images)]
-
+
+    fetch_weight.wait()
     u = embedding[...].astype(F32)
     temb = (u / (1.0 + jnp.exp(-u))).astype(BF16)
     proj = lax.dot_general(temb, weight[...], (((1,), (1,)), ((), ())), preferred_element_type=F32)
     norm[0, pl.ds(5, 2)] = proj
     fetch_kernels.wait()
 
-    def middle(first, one, two, send, recv):
+    def middle(first, one, two, at):
         for copy in first:
             copy.wait()
         mean, spread = combine(one, float(count))
-        two[0, pl.ds(0, 2)] = mean
-        two[0, pl.ds(2, 2)] = spread
-        return start_exchange(two, send, recv, second_peers())
-
-    def finish(second, two, which):
+        half = mean.shape[0]
+        two[0, pl.ds(0, half)] = mean
+        two[0, pl.ds(half, half)] = spread
+        return start_exchange(two, x_send.at[at], x_recv.at[at], second_peers())
+
+    def finish(second, two, which, image):
         for copy in second:
             copy.wait()
         mean, spread = combine(two, float(count * 2 * Y))
+        half = mean.shape[0]
         center, scale, offset = finish_norm(
-            mean, spread, float(count * 2 * Y * Z), gain[pl.ds(which, 1)], shift[pl.ds(which, 1)]
+            mean, spread, float(count * 2 * Y * Z), gain[pl.ds(which, 1)], shift[pl.ds(which, 1)], groups[...]
         )
-        norm[which, pl.ds(0, 2)] = center
-        norm[which, pl.ds(2, 2)] = scale
+        norm[which, pl.ds(image, half)] = center
+        norm[which, pl.ds(2 + image, half)] = scale
         norm[which, pl.ds(4, 1)] = offset
 
-    second = middle(first, one, two, x_send.at[1], x_recv.at[1])
+    second = middle(first, one, two, 1)
+    borders = [start_borders(own, top, bot, col, i, edge_send, edge_recv) for i in range(images)]
     for copy in bank:
         copy.wait()
     chosen = held[bank_row[image_adapter[0, owner]]]
-    lora[0, owner, patch] = chosen[0]
-    lora[1, owner, patch] = chosen[1]
-    pieces = [send_pieces(lora.at[0], lora_send.at[0], lora_recv.at[0])]
+    lora[0, owner, z, y] = chosen[0]
+    lora[1, owner, z, y] = chosen[1]
+    pieces = [send_near(lora.at[0], lora_send.at[0], lora_recv.at[0])]
     for which in range(2):
         for d in range(3):
             last = kernels[which, d, :, pl.ds(256, chans - 256)].astype(F32)
             base[which, d] = jnp.concatenate([last, jnp.zeros_like(last)], axis=1).astype(BF16)
-    finish(second, two, 0)
+    finish(second, two, 0, 0)
+    send_far(pieces[0], lora.at[0], lora_send.at[0], lora_recv.at[0])
+    pieces.append(send_near(lora.at[1], lora_send.at[1], lora_recv.at[1]))
     for copies in borders:
         wait_borders(copies)
 
     part = rows // 2
     size = part * columns
-    order = (owner, 1 - owner)
-
-    def main_dots(image):
-        def chunk(c, carry):
-            window = windows(wide, image, c * part, part)
-            total[image, pl.ds(pl.multiple_of(c * size, size), size), MAIN] = dots(window, kernels.at[0], MAIN)
-            return carry
-
-        lax.fori_loop(0, 2, chunk, 0)
-
-    for step, image in enumerate(order):
-        widen_image(own, top, bot, col, norm.at[0], image, wide, rem)
-        main_dots(image)
-        if step == 0:
-            pieces.append(send_pieces(lora.at[1], lora_send.at[1], lora_recv.at[1]))
-
-    def adapter(which, step, relay):
-        if step == 0:
-            for copy in pieces[which]:
-                copy.wait()
-            block = lora.at[which, owner]
-            relay = remote(block, block, relay_send.at[which], relay_recv.at[which], (patch, req, 1 - owner))
-            relay.start()
-        else:
-            relay.wait()
-        image = order[step]
+
+    def main_chunk(image, c):
+        window = windows(wide, image, c * part, part)
+        total[image, pl.ds(c * size, size), MAIN] = dots(window, kernels.at[0], MAIN)
+
+    def relay(which):
+        for copy in pieces[which].values():
+            copy.wait()
+        block = lora.at[which, owner]
+        copy = remote(block, block, relay_send.at[which], relay_recv.at[which], (patch, req, 1 - owner))
+        copy.start()
+        return copy
+
+    def adapter(which, image, copy):
+        pl.when(owner != image)(copy.wait)
         lay_adapter(
             lora.at[which], image, base.at[which], tail.at[image], expand.at[image], flat, ups, wide_up
         )
-        return relay
-
-    borders, relay = [], None
-    for step, image in enumerate(order):
-        relay = adapter(0, step, relay)
-
-        def chunk(c, carry, image=image):
-            at = c * part
-            window = windows(wide, image, at, part)
-            span = pl.ds(pl.multiple_of(c * size, size), size)
-            last = dots(window, tail.at[image], pl.ds(0, 128))
-            small = last.astype(BF16)
-            total[image, span, REST] = last + jnp.dot(small, expand[image, :, REST], preferred_element_type=F32)
-            total[image, span, MAIN] += jnp.dot(small, expand[image, :, MAIN], preferred_element_type=F32)
-            bias = norm[0, pl.ds(5 + image, 1)]
-            for r in range(part):
-                value = total[image, pl.ds(pl.multiple_of((at + r) * columns, columns), columns), pl.ds(0, chans)]
-                hidden[image, at + r] = (value + bias).astype(BF16)
-            return carry
-
-        lax.fori_loop(0, 2, chunk, 0)
-        borders.append(start_borders(hidden, top2, bot2, col2, image, edge2_send, edge2_recv))
-        stats(hidden, image, one2)
-
-    first = start_exchange(one2, x_send.at[2], x_recv.at[2], first_peers())
-    relay = adapter(1, 0, None)
-    second = middle(first, one2, two2, x_send.at[3], x_recv.at[3])
-    adapter(1, 1, relay)
-    finish(second, two2, 1)
-    for copies in borders:
-        wait_borders(copies)
-
-    for image in order:
+
+    def tail_chunk(image, c):
+        window = windows(wide, image, c * part, part)
+        span = pl.ds(c * size, size)
+        last = dots(window, tail.at[image], pl.ds(0, 128))
+        small = last.astype(BF16)
+        total[image, span, REST] = last + jnp.dot(small, expand[image, :, REST], preferred_element_type=F32)
+        total[image, span, MAIN] += jnp.dot(small, expand[image, :, MAIN], preferred_element_type=F32)
+        bias = norm[0, pl.ds(5 + image, 1)]
+        for r in range(c * part, c * part + part):
+            value = total[image, pl.ds(r * columns, columns), pl.ds(0, chans)]
+            hidden[image, r] = (value + bias).astype(BF16)
+
+    def hidden_done(image):
+        mean, spread = local_stats(lambda r: hidden[image, r], rows)
+        one2[image, 0, pl.ds(0, 1)] = mean
+        one2[image, 0, pl.ds(1, 1)] = spread
+        first = start_exchange(one2.at[image], x_send.at[2 + image], x_recv.at[2 + image], first_peers())
+        borders = start_borders(hidden, top2, bot2, col2, image, edge2_send, edge2_recv)
+        return first, borders
+
+    widen_image(own, top, bot, col, norm.at[0], 0, wide, rem)
+    main_chunk(0, 0)
+    main_chunk(0, 1)
+    send_far(pieces[1], lora.at[1], lora_send.at[1], lora_recv.at[1])
+    widen_image(own, top, bot, col, norm.at[0], 1, wide, rem)
+    main_chunk(1, 0)
+    relay0 = relay(0)
+    main_chunk(1, 1)
+
+    adapter(0, 0, relay0)
+    tail_chunk(0, 0)
+    tail_chunk(0, 1)
+    first0, borders0 = hidden_done(0)
+    adapter(0, 1, relay0)
+    tail_chunk(1, 0)
+    second0 = middle(first0, one2.at[0], two2.at[0], 4)
+    tail_chunk(1, 1)
+    first1, borders1 = hidden_done(1)
+    relay1 = relay(1)
+    adapter(1, 0, relay1)
+    finish(second0, two2.at[0], 1, 0)
+    wait_borders(borders0)
+    second1 = middle(first1, one2.at[1], two2.at[1], 5)
+
+    def final_chunk(image, c):
+        window = windows(wide, image, c * part, part)
+        last = dots(window, tail.at[image], pl.ds(0, 128))
+        small = last.astype(BF16)
+        body = dots(window, kernels.at[1], MAIN)
+        span = pl.ds(c * size, size)
+        total[image, span, MAIN] = body + jnp.dot(small, expand[image, :, MAIN], preferred_element_type=F32)
+        total[image, span, REST] = last + jnp.dot(small, expand[image, :, REST], preferred_element_type=F32)
+        for r in range(c * part, c * part + part):
+            value = total[image, pl.ds(r * columns, columns), pl.ds(0, chans)]
+            out[image, r] = (value + own[image, r].astype(F32)).astype(BF16)
+
+    for image in range(images):
+        if image == 1:
+            adapter(1, 1, relay1)
+            finish(second1, two2.at[1], 1, 1)
+            wait_borders(borders1)
         widen_image(hidden, top2, bot2, col2, norm.at[1], image, wide, rem)
-
-        def chunk(c, carry, image=image):
-            at = c * part
-            window = windows(wide, image, at, part)
-            last = dots(window, tail.at[image], pl.ds(0, 128))
-            small = last.astype(BF16)
-            body = dots(window, kernels.at[1], MAIN)
-            span = pl.ds(pl.multiple_of(c * size, size), size)
-            total[image, span, MAIN] = body + jnp.dot(small, expand[image, :, MAIN], preferred_element_type=F32)
-            total[image, span, REST] = last + jnp.dot(small, expand[image, :, REST], preferred_element_type=F32)
-            for r in range(part):
-                value = total[image, pl.ds(pl.multiple_of((at + r) * columns, columns), columns), pl.ds(0, chans)]
-                out[image, at + r] = (value + own[image, at + r].astype(F32)).astype(BF16)
-            return carry
-
-        lax.fori_loop(0, 2, chunk, 0)
+        final_chunk(image, 0)
+        final_chunk(image, 1)
 
 
 VM = pl.BlockSpec(memory_space=pltpu.VMEM)
@@ -468,10 +506,12 @@
     return pl.pallas_call(
         block_kernel,
         out_shape=jax.ShapeDtypeStruct(map_of, BF16),
-        in_specs=[HB, VM, VM, SM, SM, VM, VM, VM, VM, HB],
+        in_specs=[HB, VM, VM, SM, SM, VM, HB, VM, VM, HB],
         out_specs=VM,
         scratch_shapes=[
             pltpu.VMEM((images, rows, chans, columns), BF16),
+            pltpu.VMEM((chans, embedding_weight.shape[0]), BF16),
+            pltpu.VMEM((chans, chans), BF16),
             pltpu.VMEM(map_of, BF16),
             pltpu.VMEM(map_of, BF16),
             pltpu.VMEM((2, 3, 3 * chans, chans), BF16),
@@ -486,20 +526,23 @@
             pltpu.VMEM((16, chans), F32),
             pltpu.VMEM((2, deep, 128), F32),
             pltpu.VMEM((8, 2, deep, 128), BF16),
-            pltpu.VMEM((2, images, pieces, deep, 128), BF16),
+            pltpu.VMEM((2, images, Z, Y, deep, 128), BF16),
             *([line, line, edge] * 2),
             pltpu.VMEM((2, 8, chans), F32),
-            *([pltpu.VMEM((2 * Y, 8, chans), F32), pltpu.VMEM((Z, 8, chans), F32)] * 2),
-            DMA((2,)),
+            pltpu.VMEM((2 * Y, 4, chans), F32),
+            pltpu.VMEM((Z, 4, chans), F32),
+            pltpu.VMEM((images, 2 * Y, 2, chans), F32),
+            pltpu.VMEM((images, Z, 2, chans), F32),
+            DMA((3,)),
             DMA((8,)),
             DMA((8,)),
-            DMA((2, pieces)),
-            DMA((2, pieces)),
+            DMA((2, 24)),
+            DMA((2, 24)),
             DMA((2,)),
             DMA((2,)),
             *([DMA((images, 5))] * 4),
-            DMA((4, 8)),
-            DMA((4, 8)),
+            DMA((6, 8)),
+            DMA((6, 8)),
         ],
         compiler_params=pltpu.CompilerParams(
             collective_id=0, has_side_effects=True, vmem_limit_bytes=56 * 2**20

time: 74.6 us -> 77.9 us (1.044)
  Pallas kernels: 71.2 us -> 75.2 us
    pallas_call x1, Pallas kernels: 71.2 us -> 75.2 us  [local(): pl.pallas_call(block_kernel, out_shape=jax.ShapeDtypeStruct(map_of, BF16)...]
where the time goes in v3:
time: 77.9 us; the launch traced here: 77.7 us
  Pallas kernels  75.2 us (97%)
  local copies, waits for them, and re-layouts  2.53 us (3%)
    pallas_call x1, Pallas kernels, local(): pl.pallas_call(block_kernel, out_shape=jax.ShapeDtypeStruct(map_of, BF16)...  75.2 us
    pallas_call x1, local copies, waits for them, and re-layouts, local(): pl.pallas_call(block_kernel, out_shape=jax.ShapeDtypeStruct(map_of, BF16)...  2.53 us

profile of v3, /device:TPU:1, one launch (start us, length us, event | category | flops | bytes accessed | tf_op | source)
XLA Modules:
  0.0 77.7 jit_solution(408110629456269089)
XLA Ops:
  0.0 75.2 %resnet_block.1 = bf16[2,8,128,320]{3,2,1,0:T(8,128)(2,1)} custom-call(bf16[2,8,320,128]{3,2,1,0:T(8,128)(2,1)} %bitcast.5, bf16[1,2,5760]{2,1,0:T(2,128)(2,1)} %reduce_row.1, bf16[1,2,640]{2,1,0:T(2,128)(2,1)} %expand_row.1, s32[1,2]{1,0:T(1,128)} %bitcast.7, s32[8]{0:T(128)} %bank_row.1, bf16[2,1280]{1,0:T(2,128)(2,1)} %embedding.1, ...), custom_call_target="tpu_custom_call" | custom-call | tf_op jit(solution)/shard_map/resnet_block/pallas_call | solution.py:506
  75.2 2.5 %copy.11 = bf16[2,8,128,320]{2,3,1,0:T(8,128)(2,1)} copy(bf16[2,8,128,320]{3,2,1,0:T(8,128)(2,1)} %resnet_block.1) | data formatting | bytes 2621440 | tf_op jit(solution)/shard_map/resnet_block/pallas_call | solution.py:506

commit v4 on v3

--- a/solution.py
+++ b/solution.py
@@ -24,16 +24,6 @@
     return patch, req, owner, patch // Z, patch % Z
 
 
-def near():
-    patch, req, owner, y, z = place()
-    return [
-        (dz, dy, ((y + dy) % Y * Z + (z + dz) % Z, req, owner))
-        for dz in (2, -2, 1, -1, 0)
-        for dy in range(Y)
-        if dz or dy
-    ]
-
-
 def greet():
     patch, req, owner, y, z = place()
     sem = pltpu.get_barrier_semaphore()
@@ -42,19 +32,20 @@
     def signal(device):
         pl.semaphore_signal(sem, inc=1, device_id=device, device_id_type=MESH)
 
-    for _, _, device in near():
-        signal(device)
+    for dz in range(1, Z):
+        signal((y * Z + (z + dz) % Z, req, owner))
         count += 1
-    for dz in range(3, Z - 2):
-        signal((y * Z + (z + dz) % Z, req, owner))
+    for dy in range(1, Y):
+        signal(((y + dy) % Y * Z + z, req, owner))
         count += 1
     for k in range(1, 2 * Y, 2):
         g = (y * 2 + owner + k) % (2 * Y)
         signal(((g // 2) * Z + z, req, g % 2))
         count += 1
     for step in (1, Y * Z - 1):
-        signal(((patch + step) % (Y * Z), req, 1 - owner))
-        count += 1
+        for other in (owner, 1 - owner):
+            signal(((patch + step) % (Y * Z), req, other))
+            count += 1
     for k in range(1, 8):
         g = (req * 2 + owner + k) % 8
         signal((patch, g // 2, g % 2))
@@ -106,8 +97,7 @@
 def wait_borders(copies):
     for sends, receives, copy in copies:
         if sends is None:
-            copy.wait_send()
-            copy.wait_recv()
+            copy.wait()
         else:
             pl.when(sends)(copy.wait_send)
             pl.when(receives)(copy.wait_recv)
@@ -199,34 +189,29 @@
     return piece[...].astype(BF16)
 
 
-def send_near(lora, send, recv):
-    patch, req, owner, y, z = place()
-    block = lora.at[owner, z, y]
-    copies = {}
-    for k, (dz, dy, device) in enumerate(near()):
-        copies[dz, dy] = remote(block, block, send.at[k], recv.at[k], device)
-        copies[dz, dy].start()
+def send_along_z(lora, send, recv):
+    patch, req, owner, y, z = place()
+    block = lora.at[owner, y, z]
+    copies = [
+        remote(block, block, send.at[k], recv.at[k], (y * Z + (z + k) % Z, req, owner)) for k in range(1, Z)
+    ]
+    for copy in copies:
+        copy.start()
     return copies
 
 
-def send_far(copies, lora, send, recv):
-    patch, req, owner, y, z = place()
-    half = Y // 2
-
-    def forward(at, column, ys, dz):
-        block = lora.at[owner, column, ys]
-        copy = remote(block, block, send.at[at], recv.at[at], (y * Z + (z + dz) % Z, req, owner))
+def send_along_y(copies, lora, send, recv):
+    patch, req, owner, y, z = place()
+    for copy in copies:
+        copy.wait()
+    block = lora.at[owner, y]
+    copies = [
+        remote(block, block, send.at[Z + k], recv.at[Z + k], ((y + k) % Y * Z + z, req, owner))
+        for k in (2, 1, 3)
+    ]
+    for copy in copies:
         copy.start()
-        copies[at] = copy
-
-    for dz in (2, -2):
-        for dy in range(Y):
-            copies.pop((dz, dy)).wait()
-    below, above = (z + Z - 2) % Z, (z + 2) % Z
-    forward(20, below, pl.ds(0, Y), 1)
-    forward(21, above, pl.ds(0, Y), Z - 1)
-    forward(22, below, pl.ds(0, half), 2)
-    forward(23, above, pl.ds(half, half), Z - 2)
+    return copies
 
 
 def lay_adapter(lora, image, base, tail, expand, flat, ups, wide_up):
@@ -235,7 +220,7 @@
     half = depth // 2
 
     def lay(p, carry):
-        value = lora[image, p % Z, p // Z].astype(F32)
+        value = lora[image, p // Z, p % Z].astype(F32)
         down = value[0:half]
         flat[pl.ds(p * depth, half, 2)] = pltpu.roll(down, 64, 1)
         flat[pl.ds(p * depth + 1, half, 2)] = down
@@ -259,13 +244,11 @@
         expand[:, pl.ds(b * 128, 128)] = wide_up[...].astype(BF16)
 
 
-def widen_image(source, top, bot, col, norm, image, wide, rem):
+def widen_image(source, top, bot, col, norm, image, wide, rem, inner):
     patch, req, owner, y, z = place()
     rows, columns = source.shape[1:3]
     last = Y * Z - 1
     index = lax.broadcasted_iota(jnp.int32, (columns, 1), 0)
-    across = lax.broadcasted_iota(jnp.int32, (rows + 2, 1), 0)
-    beyond = ((patch > 0) | (across > 0)) & ((patch < last) | (across < rows + 1))
     center = norm[pl.ds(image, 1)]
     scale = norm[pl.ds(2 + image, 1)]
     offset = norm[pl.ds(4, 1)]
@@ -274,30 +257,40 @@
         h = (x.astype(F32) - center) * scale + offset
         return h + h * jnp.tanh(h)
 
-    border = jnp.where(owner == 0, col[image, :, 0, :].astype(F32), col[image, :, EDGE - 1, :].astype(F32))
-    rem[pl.ds(0, rows + 2)] = jnp.where(beyond, activate(border), 0.0)
-
-    def lay(r, act):
-        edge = rem[pl.ds(r, 1)]
+    def border(at):
+        return activate(
+            jnp.where(owner == 0, col[image, at, 0, :].astype(F32), col[image, at, EDGE - 1, :].astype(F32))
+        )
+
+    def lay(r, act, edge):
         left = jnp.where(index == 0, jnp.where(owner == 1, edge, 0.0), pltpu.roll(act, 1, 0))
         right = jnp.where(
             index == columns - 1, jnp.where(owner == 0, edge, 0.0), pltpu.roll(act, columns - 1, 0)
         )
         wide[image, r] = jnp.concatenate([left, act, right], axis=1).astype(BF16)
 
-    lay(0, jnp.where(patch > 0, activate(top[image]), 0.0))
-    lay(rows + 1, jnp.where(patch < last, activate(bot[image]), 0.0))
-
-    def row(r, carry):
-        lay(r + 1, activate(source[image, r]))
-        return carry
-
-    lax.fori_loop(0, rows, row, 0)
+    if inner:
+        rem[pl.ds(0, rows)] = border(slice(1, rows + 1))
+
+        def row(r, carry):
+            lay(r + 1, activate(source[image, r]), rem[pl.ds(r, 1)])
+            return carry
+
+        lax.fori_loop(0, rows, row, 0)
+    else:
+        for r, block, inside in ((0, top, patch > 0), (rows + 1, bot, patch < last)):
+            edge = jnp.where(inside, border(slice(r, r + 1)), 0.0)
+            lay(r, jnp.where(inside, activate(block[image]), 0.0), edge)
 
 
 def windows(wide, image, at, part):
     columns, depth = wide.shape[2:]
     return [wide[image, pl.ds(at + d, part)].reshape(part * columns, depth) for d in range(3)]
+
+
+def edge_windows(wide, image):
+    last = wide.shape[1] - 3
+    return [jnp.concatenate([wide[image, d], wide[image, last + d]], axis=0) for d in range(3)]
 
 
 def dots(window, matrix, lanes):
@@ -383,108 +376,131 @@
         norm[which, pl.ds(4, 1)] = offset
 
     second = middle(first, one, two, 1)
-    borders = [start_borders(own, top, bot, col, i, edge_send, edge_recv) for i in range(images)]
     for copy in bank:
         copy.wait()
     chosen = held[bank_row[image_adapter[0, owner]]]
-    lora[0, owner, z, y] = chosen[0]
-    lora[1, owner, z, y] = chosen[1]
-    pieces = [send_near(lora.at[0], lora_send.at[0], lora_recv.at[0])]
+    lora[0, owner, y, z] = chosen[0]
+    lora[1, owner, y, z] = chosen[1]
+    pieces = [send_along_z(lora.at[0], lora_send.at[0], lora_recv.at[0])]
+    borders = [start_borders(own, top, bot, col, i, edge_send, edge_recv) for i in range(images)]
     for which in range(2):
         for d in range(3):
             last = kernels[which, d, :, pl.ds(256, chans - 256)].astype(F32)
             base[which, d] = jnp.concatenate([last, jnp.zeros_like(last)], axis=1).astype(BF16)
     finish(second, two, 0, 0)
-    send_far(pieces[0], lora.at[0], lora_send.at[0], lora_recv.at[0])
-    pieces.append(send_near(lora.at[1], lora_send.at[1], lora_recv.at[1]))
-    for copies in borders:
-        wait_borders(copies)
-
-    part = rows // 2
-    size = part * columns
-
-    def main_chunk(image, c):
-        window = windows(wide, image, c * part, part)
-        total[image, pl.ds(c * size, size), MAIN] = dots(window, kernels.at[0], MAIN)
+    pieces[0] = send_along_y(pieces[0], lora.at[0], lora_send.at[0], lora_recv.at[0])
+
+    order = (owner, 1 - owner)
+    inner = (rows - 2) // 2
+    ends = (0, rows - 1)
+
+    def pixels(r, count=1):
+        return pl.ds(pl.multiple_of(r * columns, columns), count * columns)
+
+    def main_inner(image):
+        def chunk(c, carry):
+            at = 1 + c * inner
+            total[image, pixels(at, inner), MAIN] = dots(windows(wide, image, at, inner), kernels.at[0], MAIN)
+            return carry
+
+        lax.fori_loop(0, 2, chunk, 0)
+
+    def main_edges(image):
+        value = dots(edge_windows(wide, image), kernels.at[0], MAIN)
+        for i, r in enumerate(ends):
+            total[image, pixels(r), MAIN] = value[i * columns : (i + 1) * columns]
 
     def relay(which):
-        for copy in pieces[which].values():
+        for copy in pieces[which]:
             copy.wait()
         block = lora.at[which, owner]
         copy = remote(block, block, relay_send.at[which], relay_recv.at[which], (patch, req, 1 - owner))
         copy.start()
         return copy
 
-    def adapter(which, image, copy):
-        pl.when(owner != image)(copy.wait)
+    def adapter(which, image):
         lay_adapter(
             lora.at[which], image, base.at[which], tail.at[image], expand.at[image], flat, ups, wide_up
         )
 
-    def tail_chunk(image, c):
-        window = windows(wide, image, c * part, part)
-        span = pl.ds(c * size, size)
-        last = dots(window, tail.at[image], pl.ds(0, 128))
-        small = last.astype(BF16)
-        total[image, span, REST] = last + jnp.dot(small, expand[image, :, REST], preferred_element_type=F32)
-        total[image, span, MAIN] += jnp.dot(small, expand[image, :, MAIN], preferred_element_type=F32)
-        bias = norm[0, pl.ds(5 + image, 1)]
-        for r in range(c * part, c * part + part):
-            value = total[image, pl.ds(r * columns, columns), pl.ds(0, chans)]
-            hidden[image, r] = (value + bias).astype(BF16)
-
-    def hidden_done(image):
-        mean, spread = local_stats(lambda r: hidden[image, r], rows)
-        one2[image, 0, pl.ds(0, 1)] = mean
-        one2[image, 0, pl.ds(1, 1)] = spread
-        first = start_exchange(one2.at[image], x_send.at[2 + image], x_recv.at[2 + image], first_peers())
-        borders = start_borders(hidden, top2, bot2, col2, image, edge2_send, edge2_recv)
-        return first, borders
-
-    widen_image(own, top, bot, col, norm.at[0], 0, wide, rem)
-    main_chunk(0, 0)
-    main_chunk(0, 1)
-    send_far(pieces[1], lora.at[1], lora_send.at[1], lora_recv.at[1])
-    widen_image(own, top, bot, col, norm.at[0], 1, wide, rem)
-    main_chunk(1, 0)
-    relay0 = relay(0)
-    main_chunk(1, 1)
-
-    adapter(0, 0, relay0)
-    tail_chunk(0, 0)
-    tail_chunk(0, 1)
-    first0, borders0 = hidden_done(0)
-    adapter(0, 1, relay0)
-    tail_chunk(1, 0)
-    second0 = middle(first0, one2.at[0], two2.at[0], 4)
-    tail_chunk(1, 1)
-    first1, borders1 = hidden_done(1)
-    relay1 = relay(1)
-    adapter(1, 0, relay1)
-    finish(second0, two2.at[0], 1, 0)
-    wait_borders(borders0)
-    second1 = middle(first1, one2.at[1], two2.at[1], 5)
-
-    def final_chunk(image, c):
-        window = windows(wide, image, c * part, part)
+    def tail_dots(image):
+        part = rows // 2
+
+        def chunk(c, carry):
+            at = c * part
+            last = dots(windows(wide, image, at, part), tail.at[image], pl.ds(0, 128))
+            small = last.astype(BF16)
+            span = pixels(at, part)
+            total[image, span, REST] = last + jnp.dot(small, expand[image, :, REST], preferred_element_type=F32)
+            total[image, span, MAIN] += jnp.dot(small, expand[image, :, MAIN], preferred_element_type=F32)
+            bias = norm[0, pl.ds(5 + image, 1)]
+            for r in range(part):
+                hidden[image, at + r] = (total[image, pixels(at + r), pl.ds(0, chans)] + bias).astype(BF16)
+            return carry
+
+        lax.fori_loop(0, 2, chunk, 0)
+
+    for copies in borders:
+        wait_borders(copies[4:])
+    for step, image in enumerate(order):
+        widen_image(own, top, bot, col, norm.at[0], image, wide, rem, True)
+        main_inner(image)
+        if step == 0:
+            pieces.append(send_along_z(lora.at[1], lora_send.at[1], lora_recv.at[1]))
+    for copies in borders:
+        wait_borders(copies[:4])
+    for image in order:
+        widen_image(own, top, bot, col, norm.at[0], image, wide, rem, False)
+        main_edges(image)
+    pieces[1] = send_along_y(pieces[1], lora.at[1], lora_send.at[1], lora_recv.at[1])
+
+    copy = relay(0)
+    borders = []
+    for step, image in enumerate(order):
+        if step == 1:
+            copy.wait()
+        adapter(0, image)
+        tail_dots(image)
+        borders.append(start_borders(hidden, top2, bot2, col2, image, edge2_send, edge2_recv))
+        mean, spread = local_stats(lambda r, image=image: hidden[image, r], rows)
+        one2[0, pl.ds(image, 1)] = mean
+        one2[0, pl.ds(2 + image, 1)] = spread
+
+    first = start_exchange(one2, x_send.at[2], x_recv.at[2], first_peers())
+    copy = relay(1)
+    adapter(1, order[0])
+    second = middle(first, one2, two2, 3)
+    copy.wait()
+    adapter(1, order[1])
+    finish(second, two2, 1, 0)
+
+    def final(image, window, at, rows_of):
         last = dots(window, tail.at[image], pl.ds(0, 128))
         small = last.astype(BF16)
         body = dots(window, kernels.at[1], MAIN)
-        span = pl.ds(c * size, size)
+        span = pixels(at, len(rows_of))
         total[image, span, MAIN] = body + jnp.dot(small, expand[image, :, MAIN], preferred_element_type=F32)
         total[image, span, REST] = last + jnp.dot(small, expand[image, :, REST], preferred_element_type=F32)
-        for r in range(c * part, c * part + part):
-            value = total[image, pl.ds(r * columns, columns), pl.ds(0, chans)]
+        for i, r in enumerate(rows_of):
+            value = total[image, pixels(at + i), pl.ds(0, chans)]
             out[image, r] = (value + own[image, r].astype(F32)).astype(BF16)
 
-    for image in range(images):
-        if image == 1:
-            adapter(1, 1, relay1)
-            finish(second1, two2.at[1], 1, 1)
-            wait_borders(borders1)
-        widen_image(hidden, top2, bot2, col2, norm.at[1], image, wide, rem)
-        final_chunk(image, 0)
-        final_chunk(image, 1)
+    for copies in borders:
+        wait_borders(copies[4:])
+    for image in order:
+        widen_image(hidden, top2, bot2, col2, norm.at[1], image, wide, rem, True)
+
+        def chunk(c, carry, image=image):
+            at = 1 + c * inner
+            final(image, windows(wide, image, at, inner), at, [at + i for i in range(inner)])
+            return carry
+
+        lax.fori_loop(0, 2, chunk, 0)
+    for copies in borders:
+        wait_borders(copies[:4])
+    for image in order:
+        widen_image(hidden, top2, bot2, col2, norm.at[1], image, wide, rem, False)
+        final(image, edge_windows(wide, image), 0, ends)
 
 
 VM = pl.BlockSpec(memory_space=pltpu.VMEM)
@@ -526,23 +542,23 @@
             pltpu.VMEM((16, chans), F32),
             pltpu.VMEM((2, deep, 128), F32),
             pltpu.VMEM((8, 2, deep, 128), BF16),
-            pltpu.VMEM((2, images, Z, Y, deep, 128), BF16),
+            pltpu.VMEM((2, images, Y, Z, deep, 128), BF16),
             *([line, line, edge] * 2),
             pltpu.VMEM((2, 8, chans), F32),
             pltpu.VMEM((2 * Y, 4, chans), F32),
             pltpu.VMEM((Z, 4, chans), F32),
-            pltpu.VMEM((images, 2 * Y, 2, chans), F32),
-            pltpu.VMEM((images, Z, 2, chans), F32),
+            pltpu.VMEM((2 * Y, 4, chans), F32),
+            pltpu.VMEM((Z, 4, chans), F32),
             DMA((3,)),
             DMA((8,)),
             DMA((8,)),
-            DMA((2, 24)),
-            DMA((2, 24)),
+            DMA((2, Z + Y)),
+            DMA((2, Z + Y)),
             DMA((2,)),
             DMA((2,)),
             *([DMA((images, 5))] * 4),
-            DMA((6, 8)),
-            DMA((6, 8)),
+            DMA((4, 8)),
+            DMA((4, 8)),
         ],
         compiler_params=pltpu.CompilerParams(
             collective_id=0, has_side_effects=True, vmem_limit_bytes=56 * 2**20

time: 77.9 us -> 69.6 us (0.89)
  Pallas kernels: 75.2 us -> 66.9 us
    pallas_call x1, Pallas kernels: 75.2 us -> 66.9 us  [local(): pl.pallas_call(block_kernel, out_shape=jax.ShapeDtypeStruct(map_of, BF16)...]
where the time goes in v4:
time: 69.6 us; the launch traced here: 69.5 us
  Pallas kernels  66.9 us (96%)
  local copies, waits for them, and re-layouts  2.53 us (4%)
    pallas_call x1, Pallas kernels, local(): pl.pallas_call(block_kernel, out_shape=jax.ShapeDtypeStruct(map_of, BF16)...  66.9 us
    pallas_call x1, local copies, waits for them, and re-layouts, local(): pl.pallas_call(block_kernel, out_shape=jax.ShapeDtypeStruct(map_of, BF16)...  2.53 us

profile of v4, /device:TPU:1, one launch (start us, length us, event | category | flops | bytes accessed | tf_op | source)
XLA Modules:
  0.0 69.5 jit_solution(16842913439236526650)
XLA Ops:
  0.0 66.9 %resnet_block.1 = bf16[2,8,128,320]{3,2,1,0:T(8,128)(2,1)} custom-call(bf16[2,8,320,128]{3,2,1,0:T(8,128)(2,1)} %bitcast.5, bf16[1,2,5760]{2,1,0:T(2,128)(2,1)} %reduce_row.1, bf16[1,2,640]{2,1,0:T(2,128)(2,1)} %expand_row.1, s32[1,2]{1,0:T(1,128)} %bitcast.7, s32[8]{0:T(128)} %bank_row.1, bf16[2,1280]{1,0:T(2,128)(2,1)} %embedding.1, ...), custom_call_target="tpu_custom_call" | custom-call | tf_op jit(solution)/shard_map/resnet_block/pallas_call | solution.py:522
  66.9 2.5 %copy.11 = bf16[2,8,128,320]{2,3,1,0:T(8,128)(2,1)} copy(bf16[2,8,128,320]{3,2,1,0:T(8,128)(2,1)} %resnet_block.1) | data formatting | bytes 2621440 | tf_op jit(solution)/shard_map/resnet_block/pallas_call | solution.py:522

commit v5 on v4

--- a/solution.py
+++ b/solution.py
@@ -206,11 +206,23 @@
         copy.wait()
     block = lora.at[owner, y]
     copies = [
-        remote(block, block, send.at[Z + k], recv.at[Z + k], ((y + k) % Y * Z + z, req, owner))
-        for k in (2, 1, 3)
+        remote(block, block, send.at[Z + k], recv.at[Z + k], ((y + k) % Y * Z + z, req, owner)) for k in (1, Y - 1)
     ]
     for copy in copies:
         copy.start()
+    return copies
+
+
+def forward_along_y(copies, lora, send, recv):
+    patch, req, owner, y, z = place()
+    for copy in copies:
+        copy.wait()
+    half = Z // 2
+    copies = []
+    for at, k, step in ((0, 1, 0), (Z + 2, Y - 1, half)):
+        block = lora.at[owner, (y + Y - k) % Y, pl.ds(step, half)]
+        copies.append(remote(block, block, send.at[at], recv.at[at], ((y + k) % Y * Z + z, req, owner)))
+        copies[-1].start()
     return copies
 
 
@@ -227,7 +239,7 @@
         ups[pl.ds(pl.multiple_of(p * 8, 8), 8)] = value[UP_AT : UP_AT + 8]
         return carry
 
-    lax.fori_loop(0, pieces, lay, 0)
+    lax.fori_loop(0, pieces, lay, 0, unroll=8)
     lane = lax.broadcasted_iota(jnp.int32, base.shape[1:], 1)
     for d in range(3):
         down = flat[pl.ds(d * base.shape[1], base.shape[1])]
@@ -276,7 +288,7 @@
             lay(r + 1, activate(source[image, r]), rem[pl.ds(r, 1)])
             return carry
 
-        lax.fori_loop(0, rows, row, 0)
+        lax.fori_loop(0, rows, row, 0, unroll=2)
     else:
         for r, block, inside in ((0, top, patch > 0), (rows + 1, bot, patch < last)):
             edge = jnp.where(inside, border(slice(r, r + 1)), 0.0)
@@ -331,7 +343,7 @@
         own[image, r] = jnp.transpose(raw_own[image, r].astype(F32)).astype(BF16)
         return carry
 
-    lax.fori_loop(0, images * rows, turn, 0)
+    lax.fori_loop(0, images * rows, turn, 0, unroll=4)
 
     for image in range(images):
         mean, spread = local_stats(lambda r, image=image: own[image, r], rows)
@@ -446,6 +458,7 @@
         widen_image(own, top, bot, col, norm.at[0], image, wide, rem, True)
         main_inner(image)
         if step == 0:
+            pieces[0] = forward_along_y(pieces[0], lora.at[0], lora_send.at[0], lora_recv.at[0])
             pieces.append(send_along_z(lora.at[1], lora_send.at[1], lora_recv.at[1]))
     for copies in borders:
         wait_borders(copies[:4])
@@ -461,6 +474,8 @@
             copy.wait()
         adapter(0, image)
         tail_dots(image)
+        if step == 0:
+            pieces[1] = forward_along_y(pieces[1], lora.at[1], lora_send.at[1], lora_recv.at[1])
         borders.append(start_borders(hidden, top2, bot2, col2, image, edge2_send, edge2_recv))
         mean, spread = local_stats(lambda r, image=image: hidden[image, r], rows)
         one2[0, pl.ds(image, 1)] = mean

time: 69.6 us -> 68.2 us (0.980)
  Pallas kernels: 66.9 us -> 65.5 us
    pallas_call x1, Pallas kernels: 66.9 us -> 65.5 us  [local(): pl.pallas_call(block_kernel, out_shape=jax.ShapeDtypeStruct(map_of, BF16)...]
where the time goes in v5:
time: 68.2 us; the launch traced here: 68 us
  Pallas kernels  65.5 us (96%)
  local copies, waits for them, and re-layouts  2.53 us (4%)
    pallas_call x1, Pallas kernels, local(): pl.pallas_call(block_kernel, out_shape=jax.ShapeDtypeStruct(map_of, BF16)...  65.5 us
    pallas_call x1, local copies, waits for them, and re-layouts, local(): pl.pallas_call(block_kernel, out_shape=jax.ShapeDtypeStruct(map_of, BF16)...  2.53 us

profile of v5, /device:TPU:1, one launch (start us, length us, event | category | flops | bytes accessed | tf_op | source)
XLA Modules:
  0.0 68.0 jit_solution(8772431364790427231)
XLA Ops:
  0.0 65.5 %resnet_block.1 = bf16[2,8,128,320]{3,2,1,0:T(8,128)(2,1)} custom-call(bf16[2,8,320,128]{3,2,1,0:T(8,128)(2,1)} %bitcast.5, bf16[1,2,5760]{2,1,0:T(2,128)(2,1)} %reduce_row.1, bf16[1,2,640]{2,1,0:T(2,128)(2,1)} %expand_row.1, s32[1,2]{1,0:T(1,128)} %bitcast.7, s32[8]{0:T(128)} %bank_row.1, bf16[2,1280]{1,0:T(2,128)(2,1)} %embedding.1, ...), custom_call_target="tpu_custom_call" | custom-call | tf_op jit(solution)/shard_map/resnet_block/pallas_call | solution.py:537
  65.5 2.5 %copy.11 = bf16[2,8,128,320]{2,3,1,0:T(8,128)(2,1)} copy(bf16[2,8,128,320]{3,2,1,0:T(8,128)(2,1)} %resnet_block.1) | data formatting | bytes 2621440 | tf_op jit(solution)/shard_map/resnet_block/pallas_call | solution.py:537

commit v6 on v5

--- a/solution.py
+++ b/solution.py
@@ -316,9 +316,9 @@
 def block_kernel(
     raw, reduce_row, expand_row, image_adapter, bank_row, embedding, weight_hbm, gain, shift, kernels_hbm,
     out,
-    raw_own, weight, groups, own, hidden, kernels, wide, total, base, tail, expand, flat, ups, wide_up, rem,
+    raw_own, result, weight, groups, own, hidden, kernels, wide, total, base, tail, expand, flat, ups, wide_up, rem,
     piece, held, lora, top, bot, col, top2, bot2, col2, norm, one, two, one2, two2,
-    local_sem, bank_send, bank_recv, lora_send, lora_recv, relay_send, relay_recv,
+    local_sem, out_sem, bank_send, bank_recv, lora_send, lora_recv, relay_send, relay_recv,
     edge_send, edge_recv, edge2_send, edge2_recv, x_send, x_recv,
 ):
     patch, req, owner, y, z = place()
@@ -465,7 +465,6 @@
     for image in order:
         widen_image(own, top, bot, col, norm.at[0], image, wide, rem, False)
         main_edges(image)
-    pieces[1] = send_along_y(pieces[1], lora.at[1], lora_send.at[1], lora_recv.at[1])
 
     copy = relay(0)
     borders = []
@@ -475,18 +474,17 @@
         adapter(0, image)
         tail_dots(image)
         if step == 0:
-            pieces[1] = forward_along_y(pieces[1], lora.at[1], lora_send.at[1], lora_recv.at[1])
+            pieces[1] = send_along_y(pieces[1], lora.at[1], lora_send.at[1], lora_recv.at[1])
         borders.append(start_borders(hidden, top2, bot2, col2, image, edge2_send, edge2_recv))
         mean, spread = local_stats(lambda r, image=image: hidden[image, r], rows)
         one2[0, pl.ds(image, 1)] = mean
         one2[0, pl.ds(2 + image, 1)] = spread
 
     first = start_exchange(one2, x_send.at[2], x_recv.at[2], first_peers())
+    pieces[1] = forward_along_y(pieces[1], lora.at[1], lora_send.at[1], lora_recv.at[1])
+    second = middle(first, one2, two2, 3)
     copy = relay(1)
     adapter(1, order[0])
-    second = middle(first, one2, two2, 3)
-    copy.wait()
-    adapter(1, order[1])
     finish(second, two2, 1, 0)
 
     def final(image, window, at, rows_of):
@@ -498,11 +496,22 @@
         total[image, span, REST] = last + jnp.dot(small, expand[image, :, REST], preferred_element_type=F32)
         for i, r in enumerate(rows_of):
             value = total[image, pixels(at + i), pl.ds(0, chans)]
-            out[image, r] = (value + own[image, r].astype(F32)).astype(BF16)
+            result[image, r] = (jnp.transpose(value) + raw_own[image, r].astype(F32)).astype(BF16)
 
     for copies in borders:
         wait_borders(copies[4:])
-    for image in order:
+    leaving = []
+
+    def leave(image, at, count, sem):
+        part = (image, pl.ds(at, count))
+        copy = pltpu.make_async_copy(result.at[part], out.at[part], out_sem.at[sem])
+        copy.start()
+        leaving.append(copy)
+
+    for step, image in enumerate(order):
+        if step == 1:
+            copy.wait()
+            adapter(1, image)
         widen_image(hidden, top2, bot2, col2, norm.at[1], image, wide, rem, True)
 
         def chunk(c, carry, image=image):
@@ -511,11 +520,16 @@
             return carry
 
         lax.fori_loop(0, 2, chunk, 0)
+        leave(image, 1, rows - 2, step)
     for copies in borders:
         wait_borders(copies[:4])
     for image in order:
         widen_image(hidden, top2, bot2, col2, norm.at[1], image, wide, rem, False)
         final(image, edge_windows(wide, image), 0, ends)
+        for r in ends:
+            leave(image, r, 1, len(leaving))
+    for copy in leaving:
+        copy.wait()
 
 
 VM = pl.BlockSpec(memory_space=pltpu.VMEM)
@@ -534,12 +548,13 @@
     map_of = (images, rows, columns, chans)
     line = pltpu.VMEM((images, columns, chans), BF16)
     edge = pltpu.VMEM((images, rows + 2, EDGE, chans), BF16)
-    return pl.pallas_call(
+    result = pl.pallas_call(
         block_kernel,
-        out_shape=jax.ShapeDtypeStruct(map_of, BF16),
+        out_shape=jax.ShapeDtypeStruct((images, rows, chans, columns), BF16),
         in_specs=[HB, VM, VM, SM, SM, VM, HB, VM, VM, HB],
-        out_specs=VM,
+        out_specs=HB,
         scratch_shapes=[
+            pltpu.VMEM((images, rows, chans, columns), BF16),
             pltpu.VMEM((images, rows, chans, columns), BF16),
             pltpu.VMEM((chans, embedding_weight.shape[0]), BF16),
             pltpu.VMEM((chans, chans), BF16),
@@ -565,6 +580,7 @@
             pltpu.VMEM((2 * Y, 4, chans), F32),
             pltpu.VMEM((Z, 4, chans), F32),
             DMA((3,)),
+            DMA((6,)),
             DMA((8,)),
             DMA((8,)),
             DMA((2, Z + Y)),
@@ -591,6 +607,7 @@
         shift,
         kernel_weight.reshape(2, 3, 3 * chans, chans),
     )
+    return jnp.swapaxes(result, 2, 3)
 
 
 def solution(mesh):

time: 68.2 us -> 65.8 us (0.965)
  Pallas kernels: 65.5 us -> 63.2 us
    pallas_call x1 -> x0, local copies, waits for them, and re-layouts: 2.53 us -> none  [local(): pl.pallas_call(block_kernel, out_shape=jax.ShapeDtypeStruct(map_of, BF16)...]
    unnamed x0 -> x1, local copies, waits for them, and re-layouts: none -> 2.47 us
    pallas_call x1, Pallas kernels: 65.5 us -> 63.2 us  [local(): pl.pallas_call(block_kernel, out_shape=jax.ShapeDtypeStruct((images, rows...]
where the time goes in v6:
time: 65.8 us; the launch traced here: 65.7 us
  Pallas kernels  63.2 us (96%)
  local copies, waits for them, and re-layouts  2.47 us (4%)
    pallas_call x1, Pallas kernels, local(): pl.pallas_call(block_kernel, out_shape=jax.ShapeDtypeStruct((images, rows...  63.2 us
    unnamed x1, local copies, waits for them, and re-layouts  2.47 us

profile of v6, /device:TPU:1, one launch (start us, length us, event | category | flops | bytes accessed | tf_op | source)
XLA Modules:
  0.0 65.7 jit_solution(17624597434690081581)
XLA Ops:
  0.0 63.2 %resnet_block.1 = bf16[2,8,320,128]{3,2,1,0:T(8,128)(2,1)} custom-call(bf16[2,8,320,128]{3,2,1,0:T(8,128)(2,1)} %bitcast.7, bf16[1,2,5760]{2,1,0:T(2,128)(2,1)} %reduce_row.1, bf16[1,2,640]{2,1,0:T(2,128)(2,1)} %expand_row.1, s32[1,2]{1,0:T(1,128)} %bitcast.9, s32[8]{0:T(128)} %bank_row.1, bf16[2,1280]{1,0:T(2,128)(2,1)} %embedding.1, ...), custom_call_target="tpu_custom_call" | custom-call | tf_op jit(solution)/shard_map/resnet_block/pallas_call | solution.py:551
  63.2 2.5 %copy.12 = bf16[2,8,128,320]{2,3,1,0:T(8,128)(2,1)} copy(bf16[2,8,128,320]{2,3,1,0:T(8,128)(2,1)} %bitcast.5) | data formatting | bytes 2621440

commit v7 on v6

--- a/solution.py
+++ b/solution.py
@@ -475,7 +475,8 @@
         tail_dots(image)
         if step == 0:
             pieces[1] = send_along_y(pieces[1], lora.at[1], lora_send.at[1], lora_recv.at[1])
-        borders.append(start_borders(hidden, top2, bot2, col2, image, edge2_send, edge2_recv))
+        if step == 0:
+            borders.append(start_borders(hidden, top2, bot2, col2, image, edge2_send, edge2_recv))
         mean, spread = local_stats(lambda r, image=image: hidden[image, r], rows)
         one2[0, pl.ds(image, 1)] = mean
         one2[0, pl.ds(2 + image, 1)] = spread
@@ -483,6 +484,7 @@
     first = start_exchange(one2, x_send.at[2], x_recv.at[2], first_peers())
     pieces[1] = forward_along_y(pieces[1], lora.at[1], lora_send.at[1], lora_recv.at[1])
     second = middle(first, one2, two2, 3)
+    borders.append(start_borders(hidden, top2, bot2, col2, order[1], edge2_send, edge2_recv))
     copy = relay(1)
     adapter(1, order[0])
     finish(second, two2, 1, 0)
@@ -529,6 +531,19 @@
         for r in ends:
             leave(image, r, 1, len(leaving))
     for copy in leaving:
+        copy.wait()
+
+
+def copy_out(source, target, sem):
+    images, rows = source.shape[:2]
+    copies = [
+        pltpu.make_async_copy(source.at[i, pl.ds(r, 2)], target.at[i, pl.ds(r, 2)], sem.at[i, r // 2])
+        for i in range(images)
+        for r in range(0, rows, 2)
+    ]
+    for copy in copies:
+        copy.start()
+    for copy in copies:
         copy.wait()
 
 
@@ -607,6 +622,14 @@
         shift,
         kernel_weight.reshape(2, 3, 3 * chans, chans),
     )
+    result = pl.pallas_call(
+        copy_out,
+        out_shape=jax.ShapeDtypeStruct(result.shape, BF16),
+        in_specs=[HB],
+        out_specs=HB,
+        scratch_shapes=[DMA((images, rows // 2))],
+        name="copy_out",
+    )(result)
     return jnp.swapaxes(result, 2, 3)
 
 

time: 65.8 us -> 104 us (1.58)
  Pallas kernels: 63.2 us -> 104 us
  local copies, waits for them, and re-layouts: 2.47 us -> 0 us
    pallas_call x0 -> x1, Pallas kernels: none -> 40.9 us  [local(): pl.pallas_call(copy_out, out_shape=jax.ShapeDtypeStruct(result.shape, BF1...]
    unnamed x1 -> x0, local copies, waits for them, and re-layouts: 2.47 us -> none
where the time goes in v7:
time: 104 us
  Pallas kernels  104 us (100%)
    pallas_call x1, Pallas kernels, local(): pl.pallas_call(block_kernel, out_shape=jax.ShapeDtypeStruct((images, rows...  62.7 us
    pallas_call x1, Pallas kernels, local(): pl.pallas_call(copy_out, out_shape=jax.ShapeDtypeStruct(result.shape, BF1...  40.9 us

profile of v7, /device:TPU:1, one launch (start us, length us, event | category | flops | bytes accessed | tf_op | source)
XLA Modules:
  0.0 103.8 jit_solution(11585813744280277520)
XLA Ops:
  0.0 62.7 %resnet_block.1.source = bf16[2,8,320,128]{3,2,1,0:T(8,128)(2,1)} custom-call(bf16[2,8,320,128]{3,2,1,0:T(8,128)(2,1)} %bitcast.6, bf16[1,2,5760]{2,1,0:T(2,128)(2,1)} %reduce_row.1, bf16[1,2,640]{2,1,0:T(2,128)(2,1)} %expand_row.1, s32[1,2]{1,0:T(1,128)} %bitcast.8, s32[8]{0:T(128)} %bank_row.1, bf16[2,1280]{1,0:T(2,128)(2,1)} %embedding.1, ...), custom_call_target="tpu_custom_call" | custom-call | tf_op jit(solution)/shard_map/resnet_block/pallas_call | solution.py:566
  62.7 40.9 %copy_out.1 = bf16[2,8,320,128]{3,2,1,0:T(8,128)(2,1)} custom-call(bf16[2,8,320,128]{3,2,1,0:T(8,128)(2,1)} %resnet_block.1.source), custom_call_target="tpu_custom_call" | custom-call | tf_op jit(solution)/shard_map/copy_out/pallas_call | solution.py:625

commit v8 on v6

--- a/solution.py
+++ b/solution.py
@@ -475,7 +475,8 @@
         tail_dots(image)
         if step == 0:
             pieces[1] = send_along_y(pieces[1], lora.at[1], lora_send.at[1], lora_recv.at[1])
-        borders.append(start_borders(hidden, top2, bot2, col2, image, edge2_send, edge2_recv))
+        if step == 0:
+            borders.append(start_borders(hidden, top2, bot2, col2, image, edge2_send, edge2_recv))
         mean, spread = local_stats(lambda r, image=image: hidden[image, r], rows)
         one2[0, pl.ds(image, 1)] = mean
         one2[0, pl.ds(2 + image, 1)] = spread
@@ -483,6 +484,7 @@
     first = start_exchange(one2, x_send.at[2], x_recv.at[2], first_peers())
     pieces[1] = forward_along_y(pieces[1], lora.at[1], lora_send.at[1], lora_recv.at[1])
     second = middle(first, one2, two2, 3)
+    borders.append(start_borders(hidden, top2, bot2, col2, order[1], edge2_send, edge2_recv))
     copy = relay(1)
     adapter(1, order[0])
     finish(second, two2, 1, 0)

time: 65.8 us -> 65.4 us (level)
  no operation moved by 1% of the time
where the time goes in v8:
time: 65.4 us; the launch traced here: 65.2 us
  Pallas kernels  62.7 us (96%)
  local copies, waits for them, and re-layouts  2.47 us (4%)
    pallas_call x1, Pallas kernels, local(): pl.pallas_call(block_kernel, out_shape=jax.ShapeDtypeStruct((images, rows...  62.7 us
    unnamed x1, local copies, waits for them, and re-layouts  2.47 us

profile of v8, /device:TPU:1, one launch (start us, length us, event | category | flops | bytes accessed | tf_op | source)
XLA Modules:
  0.0 65.2 jit_solution(9365454958525453523)
XLA Ops:
  0.0 62.7 %resnet_block.1 = bf16[2,8,320,128]{3,2,1,0:T(8,128)(2,1)} custom-call(bf16[2,8,320,128]{3,2,1,0:T(8,128)(2,1)} %bitcast.7, bf16[1,2,5760]{2,1,0:T(2,128)(2,1)} %reduce_row.1, bf16[1,2,640]{2,1,0:T(2,128)(2,1)} %expand_row.1, s32[1,2]{1,0:T(1,128)} %bitcast.9, s32[8]{0:T(128)} %bank_row.1, bf16[2,1280]{1,0:T(2,128)(2,1)} %embedding.1, ...), custom_call_target="tpu_custom_call" | custom-call | tf_op jit(solution)/shard_map/resnet_block/pallas_call | solution.py:553
  62.7 2.5 %copy.12 = bf16[2,8,128,320]{2,3,1,0:T(8,128)(2,1)} copy(bf16[2,8,128,320]{2,3,1,0:T(8,128)(2,1)} %bitcast.5) | data formatting | bytes 2621440

commit v9 on v8

--- a/solution.py
+++ b/solution.py
@@ -482,8 +482,8 @@
         one2[0, pl.ds(2 + image, 1)] = spread
 
     first = start_exchange(one2, x_send.at[2], x_recv.at[2], first_peers())
+    second = middle(first, one2, two2, 3)
     pieces[1] = forward_along_y(pieces[1], lora.at[1], lora_send.at[1], lora_recv.at[1])
-    second = middle(first, one2, two2, 3)
     borders.append(start_borders(hidden, top2, bot2, col2, order[1], edge2_send, edge2_recv))
     copy = relay(1)
     adapter(1, order[0])

time: 65.4 us -> 66.2 us (1.012)
  Pallas kernels: 62.7 us -> 63.5 us
    pallas_call x1, Pallas kernels: 62.7 us -> 63.5 us  [local(): pl.pallas_call(block_kernel, out_shape=jax.ShapeDtypeStruct((images, rows...]
where the time goes in v9:
time: 66.2 us; the launch traced here: 66 us
  Pallas kernels  63.5 us (96%)
  local copies, waits for them, and re-layouts  2.47 us (4%)
    pallas_call x1, Pallas kernels, local(): pl.pallas_call(block_kernel, out_shape=jax.ShapeDtypeStruct((images, rows...  63.5 us
    unnamed x1, local copies, waits for them, and re-layouts  2.47 us

profile of v9, /device:TPU:1, one launch (start us, length us, event | category | flops | bytes accessed | tf_op | source)
XLA Modules:
  0.0 66.0 jit_solution(952920170402389199)
XLA Ops:
  0.0 63.5 %resnet_block.1 = bf16[2,8,320,128]{3,2,1,0:T(8,128)(2,1)} custom-call(bf16[2,8,320,128]{3,2,1,0:T(8,128)(2,1)} %bitcast.7, bf16[1,2,5760]{2,1,0:T(2,128)(2,1)} %reduce_row.1, bf16[1,2,640]{2,1,0:T(2,128)(2,1)} %expand_row.1, s32[1,2]{1,0:T(1,128)} %bitcast.9, s32[8]{0:T(128)} %bank_row.1, bf16[2,1280]{1,0:T(2,128)(2,1)} %embedding.1, ...), custom_call_target="tpu_custom_call" | custom-call | tf_op jit(solution)/shard_map/resnet_block/pallas_call | solution.py:553
  63.5 2.5 %copy.12 = bf16[2,8,128,320]{2,3,1,0:T(8,128)(2,1)} copy(bf16[2,8,128,320]{2,3,1,0:T(8,128)(2,1)} %bitcast.5) | data formatting | bytes 2621440
